TPU v7x, 32 devices: a whole 2x2x4 slice. The times are simulated.
32 devices in a mesh: seq: 8 (over z, x), pos: 4 (over y, core).
Axes of the slice: x: 2, y: 2, z: 4, core: 2. Of those that a mesh axis runs over, the one named last changes fastest.
Arguments:
- inputs: bfloat16 [8, 1024, 768], P('seq', 'pos'), may hold values from -6 to 6
- lengths: int32 [8], P('seq'), may hold values from 64 to 1024, as said below
- prenorm: bfloat16 [2, 768], P(None, ('seq', 'pos')), may hold values from 0.099609375 to 1.8984375
- value_proj: bfloat16 [2, 768, 768], P(None, ('seq', 'pos')), may hold values from -0.21875 to 0.21875
- mixing: bfloat16 [2, 12, 1024, 1024], P(None, 'pos', 'seq'), may hold values from -8 to 8
- out_proj: bfloat16 [2, 768, 768], P(None, ('seq', 'pos')), may hold values from -1.25 to 1.25
- ffn_gain: bfloat16 [2, 768], P(None, ('seq', 'pos')), may hold values from 0.099609375 to 1.8984375
- up_proj: bfloat16 [2, 768, 3072], P(None, ('seq', 'pos')), may hold values from -0.21875 to 0.21875
- down_proj: bfloat16 [2, 3072, 768], P(None, ('seq', 'pos')), may hold values from -0.109375 to 0.109375
- cotangent: bfloat16 [8, 1024, 768], P('seq', 'pos'), may hold values from -6 to 6
Outputs:
- outputs: bfloat16 [8, 1024, 768], P('seq', 'pos')
- input_grad: bfloat16 [8, 1024, 768], P('seq', 'pos')
- grad_prenorm: float32 [2, 768], P(None, ('seq', 'pos'))
- grad_value_proj: float32 [2, 768, 768], P(None, ('seq', 'pos'))
- grad_mixing: float32 [2, 12, 1024, 1024], P(None, 'pos', 'seq')
- grad_out_proj: float32 [2, 768, 768], P(None, ('seq', 'pos'))
- grad_ffn_gain: float32 [2, 768], P(None, ('seq', 'pos'))
- grad_up_proj: float32 [2, 768, 3072], P(None, ('seq', 'pos'))
- grad_down_proj: float32 [2, 3072, 768], P(None, ('seq', 'pos'))
Inputs may be any that keep to these rules, and one draw needn't show every extreme that they name: `lengths`: some item has exactly 1024 valid positions and some exactly 64.
All inputs are finite; a program needn't handle non-finite values.
Results may differ from a plain program's by a relative error of at most 0.015.
Values may be sent and summed in bfloat16 or wider, within the bound.
A program may use at most 192 MiB of HBM per device.

v0:
```python
import jax
import jax.numpy as jnp
from jax import lax
from jax.sharding import PartitionSpec as P

epsilon = 1e-05


def rms_scale(values, gain):
    inverse = lax.rsqrt(jnp.mean(values * values, axis=-1, keepdims=True) + epsilon)
    return values * inverse * gain


def gelu_tanh(values):
    return jax.nn.gelu(values, approximate=True)


def mix_probs(logits, length):
    extent = logits.shape[-1]
    position = lax.iota(jnp.int32, extent)
    keep_column = position[None, None, :] < length
    keep_row = position[None, :, None] < length
    masked = jnp.where(keep_column, logits, -1e30)
    highest = jnp.max(masked, axis=-1, keepdims=True)
    raised = jnp.where(keep_column, jnp.exp(masked - highest), 0.0)
    shares = raised / jnp.sum(raised, axis=-1, keepdims=True)
    return jnp.where(keep_row, shares, 0.0)


def project(left, right):
    return jnp.einsum("spd,de->spe", left, right, preferred_element_type=jnp.float32)


def project_back(left, right):
    return jnp.einsum("spe,de->spd", left, right, preferred_element_type=jnp.float32)


def outer_sum(left, right):
    return jnp.einsum("spd,spe->de", left, right, preferred_element_type=jnp.float32)


def fetch_forward(which, stacked, mixing):
    gathered = (
        lax.all_gather(stacked[0][which], ("seq", "pos"), axis=0, tiled=True),
        lax.all_gather(stacked[1][which], ("seq", "pos"), axis=0, tiled=True),
        lax.all_gather(stacked[2][which], ("seq", "pos"), axis=0, tiled=True),
        lax.all_gather(stacked[3][which], ("seq", "pos"), axis=0, tiled=True),
        lax.all_gather(stacked[4][which], ("seq", "pos"), axis=0, tiled=True),
        lax.all_gather(stacked[5][which], ("seq", "pos"), axis=0, tiled=True),
    )
    logits = lax.all_gather(mixing[which], "seq", axis=1, tiled=True)
    return (gathered, logits)


def fetch_backward(which, stacked, mixing):
    gathered = (
        lax.all_gather(stacked[0][which], ("seq", "pos"), axis=0, tiled=True),
        lax.all_gather(stacked[1][which], ("seq", "pos"), axis=0, tiled=True),
        lax.all_gather(stacked[2][which], ("seq", "pos"), axis=0, tiled=True),
        lax.all_gather(stacked[3][which], ("seq", "pos"), axis=0, tiled=True),
        lax.all_gather(stacked[4][which], ("seq", "pos"), axis=0, tiled=True),
        lax.all_gather(stacked[5][which], ("seq", "pos"), axis=0, tiled=True),
    )
    logits = lax.all_gather(mixing[which], "seq", axis=1, tiled=True)
    return (gathered, logits)


def mix_forward(by_heads, logits, lengths):
    logit_values = logits.astype(jnp.float32)
    heads_here = logits.shape[0]
    seqs, slots, columns = by_heads.shape

    def per_item(pair):
        values, length = pair
        mix_weights = mix_probs(logit_values, length).astype(jnp.bfloat16)
        pieces = values.reshape(slots, heads_here, columns // heads_here)
        mixed = jnp.einsum("kij,jkd->ikd", mix_weights, pieces, preferred_element_type=jnp.float32)
        return mixed.reshape(slots, columns).astype(jnp.bfloat16)

    return lax.map(per_item, (by_heads, lengths))


def mix_backward(by_heads, grad_heads, logits, lengths):
    logit_values = logits.astype(jnp.float32)
    heads_here = logits.shape[0]
    seqs, slots, columns = by_heads.shape

    def per_item(total, triple):
        values, gradient, length = triple
        shares, pullback = jax.vjp(lambda table: mix_probs(table, length), logit_values)
        pieces = values.reshape(slots, heads_here, columns // heads_here)
        grad_pieces = gradient.reshape(slots, heads_here, columns // heads_here)
        grad_shares = jnp.einsum(
            "ikd,jkd->kij", grad_pieces, pieces, preferred_element_type=jnp.float32
        )
        grad_table = pullback(grad_shares)[0]
        grad_values = jnp.einsum(
            "kij,ikd->jkd",
            shares.astype(jnp.bfloat16),
            grad_pieces,
            preferred_element_type=jnp.float32,
        )
        return (total + grad_table, grad_values.reshape(slots, columns).astype(jnp.bfloat16))

    initial = jnp.zeros(logits.shape, jnp.float32)
    return lax.scan(per_item, initial, (by_heads, grad_heads, lengths))


def forward_layer(state, gathered, logits, lengths):
    gain, value_w, out_w, gain_ffn, up_w, down_w = gathered
    normed = rms_scale(state, gain.astype(jnp.float32)).astype(jnp.bfloat16)
    valued = project(normed, value_w).astype(jnp.bfloat16)
    by_heads = lax.all_to_all(valued, "pos", split_axis=2, concat_axis=1, tiled=True)
    mixed = mix_forward(by_heads, logits, lengths)
    returned = lax.all_to_all(mixed, "pos", split_axis=1, concat_axis=2, tiled=True)
    middle = state + project(returned, out_w)
    normed_ffn = rms_scale(middle, gain_ffn.astype(jnp.float32)).astype(jnp.bfloat16)
    activated = gelu_tanh(project(normed_ffn, up_w)).astype(jnp.bfloat16)
    return (middle + project(activated, down_w), (state, middle, normed, by_heads, returned))


def backward_layer(upstream, kept_values, gathered, logits, lengths):
    state, middle, normed, by_heads, returned = kept_values
    gain, value_w, out_w, gain_ffn, up_w, down_w = gathered
    normed_ffn, ffn_pullback = jax.vjp(rms_scale, middle, gain_ffn.astype(jnp.float32))
    normed_ffn = normed_ffn.astype(jnp.bfloat16)
    pre_act = project(normed_ffn, up_w)
    activated, gelu_pullback = jax.vjp(gelu_tanh, pre_act)
    activated = activated.astype(jnp.bfloat16)
    grad_ffn = upstream.astype(jnp.bfloat16)
    grad_down = outer_sum(activated, grad_ffn)
    grad_pre = gelu_pullback(project_back(grad_ffn, down_w))[0].astype(jnp.bfloat16)
    grad_up = outer_sum(normed_ffn, grad_pre)
    grad_mid_norm, grad_gain_ffn = ffn_pullback(project_back(grad_pre, up_w))
    grad_middle = upstream + grad_mid_norm
    grad_mid = grad_middle.astype(jnp.bfloat16)
    grad_out = outer_sum(returned, grad_mid)
    grad_mixed = project_back(grad_mid, out_w).astype(jnp.bfloat16)
    grad_heads = lax.all_to_all(grad_mixed, "pos", split_axis=2, concat_axis=1, tiled=True)
    grad_logits, grad_valued_heads = mix_backward(by_heads, grad_heads, logits, lengths)
    grad_valued = lax.all_to_all(grad_valued_heads, "pos", split_axis=1, concat_axis=2, tiled=True)
    grad_value = outer_sum(normed, grad_valued)
    first_out, first_pullback = jax.vjp(rms_scale, state, gain.astype(jnp.float32))
    grad_state_norm, grad_gain = first_pullback(project_back(grad_valued, value_w))
    terms = (grad_gain, grad_value, grad_out, grad_gain_ffn, grad_up, grad_down)
    return (grad_middle + grad_state_norm, terms, grad_logits)


def local(
    inputs, lengths, prenorm, value_proj, mixing, out_proj, ffn_gain, up_proj, down_proj, cotangent
):
    stacked = (prenorm, value_proj, out_proj, ffn_gain, up_proj, down_proj)
    layers = prenorm.shape[0]
    slots_here = inputs.shape[1]
    position = lax.axis_index("pos") * slots_here + lax.iota(jnp.int32, slots_here)
    live = (position[None, :] < lengths[:, None]).astype(jnp.float32)[:, :, None]
    state = inputs.astype(jnp.float32) * live
    fetched = []
    stored = []
    for which in range(layers):
        gathered, logits = fetch_forward(which, stacked, mixing)
        state, kept_values = forward_layer(state, gathered, logits, lengths)
        fetched.append((gathered, logits))
        stored.append(kept_values)
    upstream = cotangent.astype(jnp.float32)
    weight_grads = [None] * layers
    logit_grads = [None] * layers
    for which in reversed(range(layers)):
        gathered, logits = fetch_backward(which, stacked, mixing)
        upstream, terms, logit_terms = backward_layer(
            upstream, stored[which], gathered, logits, lengths
        )
        partial_value = (
            lax.psum_scatter(terms[0], "seq", scatter_dimension=0, tiled=True),
            lax.psum_scatter(terms[1], "seq", scatter_dimension=0, tiled=True),
            lax.psum_scatter(terms[2], "seq", scatter_dimension=0, tiled=True),
            lax.psum_scatter(terms[3], "seq", scatter_dimension=0, tiled=True),
            lax.psum_scatter(terms[4], "seq", scatter_dimension=0, tiled=True),
            lax.psum_scatter(terms[5], "seq", scatter_dimension=0, tiled=True),
        )
        weight_grads[which] = (
            lax.psum_scatter(
                partial_value[0].astype(jnp.bfloat16), "pos", scatter_dimension=0, tiled=True
            ).astype(jnp.float32),
            lax.psum_scatter(
                partial_value[1].astype(jnp.bfloat16), "pos", scatter_dimension=0, tiled=True
            ).astype(jnp.float32),
            lax.psum_scatter(
                partial_value[2].astype(jnp.bfloat16), "pos", scatter_dimension=0, tiled=True
            ).astype(jnp.float32),
            lax.psum_scatter(
                partial_value[3].astype(jnp.bfloat16), "pos", scatter_dimension=0, tiled=True
            ).astype(jnp.float32),
            lax.psum_scatter(
                partial_value[4].astype(jnp.bfloat16), "pos", scatter_dimension=0, tiled=True
            ).astype(jnp.float32),
            lax.psum_scatter(
                partial_value[5].astype(jnp.bfloat16), "pos", scatter_dimension=0, tiled=True
            ).astype(jnp.float32),
        )
        logit_grads[which] = lax.psum_scatter(logit_terms, "seq", scatter_dimension=1, tiled=True)
    merged = [
        jnp.stack([layer_terms[member] for layer_terms in weight_grads]) for member in range(6)
    ]
    merged_logits = jnp.stack(logit_grads)
    return (
        state.astype(jnp.bfloat16),
        (upstream * live).astype(jnp.bfloat16),
        merged[0],
        merged[1],
        merged_logits,
        merged[2],
        merged[3],
        merged[4],
        merged[5],
    )


def solution(mesh):
    return jax.shard_map(
        local,
        mesh=mesh,
        in_specs=(
            P("seq", "pos", None),
            P("seq"),
            P(None, ("seq", "pos")),
            P(None, ("seq", "pos"), None),
            P(None, "pos", "seq", None),
            P(None, ("seq", "pos"), None),
            P(None, ("seq", "pos")),
            P(None, ("seq", "pos"), None),
            P(None, ("seq", "pos"), None),
            P("seq", "pos", None),
        ),
        out_specs=(
            P("seq", "pos", None),
            P("seq", "pos", None),
            P(None, ("seq", "pos")),
            P(None, ("seq", "pos"), None),
            P(None, "pos", "seq", None),
            P(None, ("seq", "pos"), None),
            P(None, ("seq", "pos")),
            P(None, ("seq", "pos"), None),
            P(None, ("seq", "pos"), None),
        ),
        check_vma=False,
    )
```

profile of v0, /device:TPU:0, one launch (start us, length us, event | category | flops | bytes accessed | tf_op | source)
XLA Modules:
  0.0 2287.7 jit_solution(3834089573215488454)
XLA Ops:
  18.9 42.1 %all-reduce.13 = (bf16[768]{0:T(1024)(128)(2,1)S(1)}, bf16[768]{0:T(1024)(128)(2,1)S(1)}, bf16[768]{0:T(1024)(128)(2,1)S(1)}, bf16[768]{0:T(1024)(128)(2,1)}) all-reduce(bf16[768]{0:T(1024)(128)(2,1)S(1)} %dynamic-update-slice, bf16[768]{0:T(1024)(128)(2,1)S(1)} %dynamic-update-slice.1, ...), channel_id=2, replica_groups=mesh['seq'=8,'pos'=4] {'seq','pos'}, use_global_device_ids=true, to_apply=%add | all-reduce | flops 3072 | bytes 12288
  87.1 82.5 %all-gather.37.cloned.1.call-done = bf16[1,3,1024,1024]{2,3,1,0:T(8,128)(2,1)} async-done(((bf16[1,3,128,1024]{2,3,1,0:T(8,128)(2,1)}), bf16[1,3,1024,1024]{2,3,1,0:T(8,128)(2,1)}) %all-gather.37.cloned.1.call-update) | async-done | bytes 6291472 | tf_op jit(solution)/shard_map/all_gather | solution.py:51
  174.2 95.1 %all-gather.27.cloned.1.call-done = bf16[1,3,1024,1024]{2,3,1,0:T(8,128)(2,1)} async-done(((bf16[1,3,128,1024]{2,3,1,0:T(8,128)(2,1)}), bf16[1,3,1024,1024]{2,3,1,0:T(8,128)(2,1)}) %all-gather.27.cloned.1.call-update) | async-done | bytes 6291472 | tf_op jit(solution)/shard_map/all_gather | solution.py:51
  326.2 64.0 %all-gather.31.cloned.1.call-done = bf16[1,768,3072]{2,1,0:T(8,128)(2,1)} async-done(((bf16[1,24,3072]{2,1,0:T(8,128)(2,1)}), bf16[1,768,3072]{2,1,0:T(8,128)(2,1)}) %all-gather.31.cloned.1.call-update) | async-done | bytes 4718608 | tf_op jit(solution)/shard_map/all_gather | solution.py:48
  395.7 59.8 %all-gather.33.cloned.1.call-done = bf16[1,3072,768]{2,1,0:T(8,128)(2,1)} async-done(((bf16[1,96,768]{2,1,0:T(8,128)(2,1)}), bf16[1,3072,768]{2,1,0:T(8,128)(2,1)}) %all-gather.33.cloned.1.call-update) | async-done | bytes 4718608 | tf_op jit(solution)/shard_map/all_gather | solution.py:49
  460.8 49.9 %all-gather.35.cloned.1.call-done = bf16[1,768,768]{2,1,0:T(8,128)(2,1)} async-done(((bf16[1,24,768]{2,1,0:T(8,128)(2,1)}), bf16[1,768,768]{2,1,0:T(8,128)(2,1)}) %all-gather.35.cloned.1.call-update) | async-done | bytes 1179664 | tf_op jit(solution)/shard_map/all_gather | solution.py:45
  569.0 63.5 %all-gather.41.cloned.1.call-done = bf16[1,768,3072]{2,1,0:T(8,128)(2,1)} async-done(((bf16[1,24,3072]{2,1,0:T(8,128)(2,1)}), bf16[1,768,3072]{2,1,0:T(8,128)(2,1)}) %all-gather.41.cloned.1.call-update) | async-done | bytes 4718608 | tf_op jit(solution)/shard_map/all_gather | solution.py:48
  638.0 59.7 %all-gather.43.cloned.1.call-done = bf16[1,3072,768]{2,1,0:T(8,128)(2,1)} async-done(((bf16[1,96,768]{2,1,0:T(8,128)(2,1)}), bf16[1,3072,768]{2,1,0:T(8,128)(2,1)}) %all-gather.43.cloned.1.call-update) | async-done | bytes 4718608 | tf_op jit(solution)/shard_map/all_gather | solution.py:49
  892.4 42.7 %reduce-scatter.23.cloned.1.call-done = f32[96,768]{1,0:T(8,128)} async-done(((f32[768,768]{1,0:T(8,128)}), f32[96,768]{1,0:T(8,128)}) %reduce-scatter.23.cloned.1.call-update) | async-done | bytes 294928 | tf_op jit(solution)/shard_map/reduce_scatter | solution.py:175
  936.8 70.5 %reduce-scatter.19.cloned.1.call-done = f32[96,768]{1,0:T(8,128)} async-done(((f32[768,768]{1,0:T(8,128)}), f32[96,768]{1,0:T(8,128)}) %reduce-scatter.19.cloned.1.call-update) | async-done | bytes 294928 | tf_op jit(solution)/shard_map/reduce_scatter | solution.py:175
  1009.1 163.1 %reduce-scatter.51.cloned.1.call-done = f32[384,768]{1,0:T(8,128)} async-done(((f32[3072,768]{1,0:T(8,128)}), f32[384,768]{1,0:T(8,128)}) %reduce-scatter.51.cloned.1.call-update) | async-done | bytes 1179664 | tf_op jit(solution)/shard_map/reduce_scatter | solution.py:179
  1180.9 155.9 %reduce-scatter.47.cloned.1.call-done = f32[384,768]{1,0:T(8,128)} async-done(((f32[3072,768]{1,0:T(8,128)}), f32[384,768]{1,0:T(8,128)}) %reduce-scatter.47.cloned.1.call-update) | async-done | bytes 1179664 | tf_op jit(solution)/shard_map/reduce_scatter | solution.py:179
  1339.1 17.9 fusion.23
  1357.1 144.5 %reduce-scatter.43.cloned.1.call-done = f32[96,3072]{1,0:T(8,128)} async-done(((f32[768,3072]{1,0:T(8,128)}), f32[96,3072]{1,0:T(8,128)}) %reduce-scatter.43.cloned.1.call-update) | async-done | bytes 1179664 | tf_op jit(solution)/shard_map/reduce_scatter | solution.py:178
  1503.8 27.7 %convert_reduce_fusion.1 = (f32[3,1024]{1,0:T(4,128)S(1)}, pred[3,1024,1024]{1,2,0:T(8,128)(4,1)}, f32[3,1024]{1,0:T(4,128)S(1)}, f32[3,1024,1024]{1,2,0:T(8,128...) fusion(f32[3,1024]{1,0:T(4,128)S(1)} %copy-done.32, ...), kind=kLoop, calls=%fused_computation.29 | loop fusion | flops 75485184 | bytes 69329920 | tf_op jit(solution)/shard_map/while/body/eval_jaxpr/jvp()/reduce_sum | solution.py:24
  1531.5 134.8 %reduce-scatter.39.cloned.1.call-done = f32[96,3072]{1,0:T(8,128)} async-done(((f32[768,3072]{1,0:T(8,128)}), f32[96,3072]{1,0:T(8,128)}) %reduce-scatter.39.cloned.1.call-update) | async-done | bytes 1179664 | tf_op jit(solution)/shard_map/reduce_scatter | solution.py:178
  1668.7 21.3 add_select_fusion.1
  1700.3 35.1 %all-reduce.12 = (bf16[768]{0:T(1024)(128)(2,1)S(1)}, bf16[768]{0:T(1024)(128)(2,1)S(1)}, bf16[768]{0:T(1024)(128)(2,1)S(1)}, bf16[768]{0:T(1024)(128)(2,1)S(1)}) all-reduce(f32[768]{0:T(1024)S(1)} %copy-done.49, f32[768]{0:T(1024)S(1)} %get-tuple-element.123, ...), channel_id=18, replica_groups=mesh['seq'=8,'pos'=4] {'seq'}, use_global_device_ids=true, to_apply=%region_16.17.clone | all-reduce | flops 3072 | bytes 18432
  1756.3 23.7 %reduce-scatter.53.cloned.1.call-done = bf16[96,768]{1,0:T(8,128)(2,1)} async-done(((bf16[384,768]{1,0:T(8,128)(2,1)}), bf16[96,768]{1,0:T(8,128)(2,1)}) %reduce-scatter.53.cloned.1.call-update) | async-done | bytes 147472 | tf_op jit(solution)/shard_map/reduce_scatter | solution.py:197
  1780.0 24.4 %reduce-scatter.49.cloned.1.call-done = bf16[96,768]{1,0:T(8,128)(2,1)} async-done(((bf16[384,768]{1,0:T(8,128)(2,1)}), bf16[96,768]{1,0:T(8,128)(2,1)}) %reduce-scatter.49.cloned.1.call-update) | async-done | bytes 147472 | tf_op jit(solution)/shard_map/reduce_scatter | solution.py:197
  1806.3 23.3 %reduce-scatter.45.cloned.1.call-done = bf16[24,3072]{1,0:T(8,128)(2,1)} async-done(((bf16[96,3072]{1,0:T(8,128)(2,1)}), bf16[24,3072]{1,0:T(8,128)(2,1)}) %reduce-scatter.45.cloned.1.call-update) | async-done | bytes 147472 | tf_op jit(solution)/shard_map/reduce_scatter | solution.py:194
  1829.7 24.4 %reduce-scatter.41.cloned.1.call-done = bf16[24,3072]{1,0:T(8,128)(2,1)} async-done(((bf16[96,3072]{1,0:T(8,128)(2,1)}), bf16[24,3072]{1,0:T(8,128)(2,1)}) %reduce-scatter.41.cloned.1.call-update) | async-done | bytes 147472 | tf_op jit(solution)/shard_map/reduce_scatter | solution.py:194
  1855.9 209.5 %reduce-scatter.27.cloned.1.call-done = f32[3,128,1024]{1,2,0:T(8,128)} async-done(((f32[3,1024,1024]{1,2,0:T(8,128)}), f32[3,128,1024]{1,2,0:T(8,128)}) %reduce-scatter.27.cloned.1.call-update) | async-done | bytes 1572880 | tf_op jit(solution)/shard_map/reduce_scatter | solution.py:201
  2065.4 210.6 %reduce-scatter.29.cloned.1.call-done = f32[3,128,1024]{1,2,0:T(8,128)} async-done(((f32[3,1024,1024]{1,2,0:T(8,128)}), f32[3,128,1024]{1,2,0:T(8,128)}) %reduce-scatter.29.cloned.1.call-update) | async-done | bytes 1572880 | tf_op jit(solution)/shard_map/reduce_scatter | solution.py:201
  (369 shorter events, 423.5 us)
Async XLA Ops:
  11.5 257.9 %all-gather.27.cloned.1.call-start = ((), (), s32[]{:S(2)}) async-start(), calls=%async_computation.45 | async-start | bytes 7077888 | tf_op jit(solution)/shard_map/all_gather | solution.py:51
  12.7 311.6 %all-gather.29.cloned.1.call-start = ((), (), s32[]{:S(2)}) async-start(), calls=%async_computation.46 | async-start | bytes 1216512 | tf_op jit(solution)/shard_map/all_gather | solution.py:46
  13.4 376.8 %all-gather.31.cloned.1.call-start = ((), (), s32[]{:S(2)}) async-start(), calls=%async_computation.47 | async-start | bytes 4866048 | tf_op jit(solution)/shard_map/all_gather | solution.py:48
  14.2 441.2 %all-gather.33.cloned.1.call-start = ((), (), s32[]{:S(2)}) async-start(), calls=%async_computation.48 | async-start | bytes 4866048 | tf_op jit(solution)/shard_map/all_gather | solution.py:49
  15.1 495.6 %all-gather.35.cloned.1.call-start = ((), (), s32[]{:S(2)}) async-start(), calls=%async_computation.49 | async-start | bytes 1216512 | tf_op jit(solution)/shard_map/all_gather | solution.py:45
  15.8 550.7 %all-gather.39.cloned.1.call-start = ((), (), s32[]{:S(2)}) async-start(), calls=%async_computation.51 | async-start | bytes 1216512 | tf_op jit(solution)/shard_map/all_gather | solution.py:46
  16.6 616.0 %all-gather.41.cloned.1.call-start = ((), (), s32[]{:S(2)}) async-start(), calls=%async_computation.52 | async-start | bytes 4866048 | tf_op jit(solution)/shard_map/all_gather | solution.py:48
  78.7 619.1 %all-gather.43.cloned.1.call-start = ((), (), s32[]{:S(2)}) async-start(), calls=%async_computation.53 | async-start | bytes 4866048 | tf_op jit(solution)/shard_map/all_gather | solution.py:49
  541.4 347.5 %reduce-scatter.35.cloned.1.call-start = ((), (), s32[]{:S(2)}) async-start(), calls=%async_computation.34 | async-start | bytes 2654208 | tf_op jit(solution)/shard_map/reduce_scatter | solution.py:176
  798.0 209.4 %reduce-scatter.19.cloned.1.call-start = ((), (), s32[]{:S(2)}) async-start(), calls=%async_computation.26 | async-start | bytes 2654208 | tf_op jit(solution)/shard_map/reduce_scatter | solution.py:175
  857.6 314.5 %reduce-scatter.51.cloned.1.call-start = ((), (), s32[]{:S(2)}) async-start(), calls=%async_computation.42 | async-start | bytes 10616832 | tf_op jit(solution)/shard_map/reduce_scatter | solution.py:179
  865.5 471.4 %reduce-scatter.47.cloned.1.call-start = ((), (), s32[]{:S(2)}) async-start(), calls=%async_computation.40 | async-start | bytes 10616832 | tf_op jit(solution)/shard_map/reduce_scatter | solution.py:179
  874.4 627.1 %reduce-scatter.43.cloned.1.call-start = ((), (), s32[]{:S(2)}) async-start(), calls=%async_computation.38 | async-start | bytes 10616832 | tf_op jit(solution)/shard_map/reduce_scatter | solution.py:178
  881.6 784.6 %reduce-scatter.39.cloned.1.call-start = ((), (), s32[]{:S(2)}) async-start(), calls=%async_computation.36 | async-start | bytes 10616832 | tf_op jit(solution)/shard_map/reduce_scatter | solution.py:178
  888.8 854.9 %reduce-scatter.37.cloned.1.call-start = ((), (), s32[]{:S(2)}) async-start(), calls=%async_computation.35 | async-start | bytes 184320 | tf_op jit(solution)/shard_map/reduce_scatter | solution.py:188
  890.6 853.1 %reduce-scatter.33.cloned.1.call-start = ((), (), s32[]{:S(2)}) async-start(), calls=%async_computation.33 | async-start | bytes 184320 | tf_op jit(solution)/shard_map/reduce_scatter | solution.py:188
  892.3 852.9 %reduce-scatter.25.cloned.1.call-start = ((), (), s32[]{:S(2)}) async-start(), calls=%async_computation.29 | async-start | bytes 184320 | tf_op jit(solution)/shard_map/reduce_scatter | solution.py:185
  936.8 818.1 %reduce-scatter.21.cloned.1.call-start = ((), (), s32[]{:S(2)}) async-start(), calls=%async_computation.27 | async-start | bytes 184320 | tf_op jit(solution)/shard_map/reduce_scatter | solution.py:185
  1009.0 771.0 %reduce-scatter.53.cloned.1.call-start = ((), (), s32[]{:S(2)}) async-start(), calls=%async_computation.43 | async-start | bytes 737280 | tf_op jit(solution)/shard_map/reduce_scatter | solution.py:197
  1174.3 630.1 %reduce-scatter.49.cloned.1.call-start = ((), (), s32[]{:S(2)}) async-start(), calls=%async_computation.41 | async-start | bytes 737280 | tf_op jit(solution)/shard_map/reduce_scatter | solution.py:197
  1339.0 490.6 %reduce-scatter.45.cloned.1.call-start = ((), (), s32[]{:S(2)}) async-start(), calls=%async_computation.39 | async-start | bytes 737280 | tf_op jit(solution)/shard_map/reduce_scatter | solution.py:194
  1503.7 350.4 %reduce-scatter.41.cloned.1.call-start = ((), (), s32[]{:S(2)}) async-start(), calls=%async_computation.37 | async-start | bytes 737280 | tf_op jit(solution)/shard_map/reduce_scatter | solution.py:194
  1668.4 397.0 %reduce-scatter.27.cloned.1.call-start = ((), (), s32[]{:S(2)}) async-start(), calls=%async_computation.30 | async-start | bytes 14155776 | tf_op jit(solution)/shard_map/reduce_scatter | solution.py:201
  1690.1 585.9 %reduce-scatter.29.cloned.1.call-start = ((), (), s32[]{:S(2)}) async-start(), calls=%async_computation.31 | async-start | bytes 14155776 | tf_op jit(solution)/shard_map/reduce_scatter | solution.py:201
  (75 other events, 3564.9 us)
Sparse Core Ops, SparseCore 0:
  11.5 56.8 all-gather.24
  71.0 98.5 all-gather.36
  171.7 97.6 all-gather.26
  272.1 52.1 all-gather.28
  327.7 62.4 all-gather.30
  393.6 61.8 all-gather.32
  458.4 52.2 all-gather.34
  513.6 52.8 all-gather.38
  570.0 62.4 all-gather.40
  635.8 61.8 all-gather.42
  709.0 67.9 reduce-scatter.34
  795.0 67.7 reduce-scatter.30
  866.3 68.7 reduce-scatter.22
  938.5 68.8 reduce-scatter.18
  1010.8 161.3 reduce-scatter.50
  1175.6 161.1 reduce-scatter.46
  1340.3 161.1 reduce-scatter.42
  1505.0 161.1 reduce-scatter.38
  1757.9 22.0 reduce-scatter.52
  1782.4 22.0 reduce-scatter.48
  1807.6 22.0 reduce-scatter.44
  1832.0 22.0 reduce-scatter.40
  1857.6 207.8 reduce-scatter.26
  2069.0 206.9 reduce-scatter.28
  (4 shorter events, 77.5 us)
where the time goes:
time: 2300 us; the launch traced here: 2290 us
  waiting for transfers between devices  1770 us (77%)
  blocking collectives  138 us (6%)
  other arithmetic  138 us (6%)
  matrix products  133 us (6%)
  local copies, waits for them, and re-layouts  79 us (3%)
    reduce_scatter x2, waiting for transfers between devices, local(): lax.psum_scatter(logit_terms, 'seq', scatter_dimension=1, tiled=True)  420 us
    reduce_scatter x2, waiting for transfers between devices, local(): lax.psum_scatter(terms[5], 'seq', scatter_dimension=0, tiled=True)  319 us
    reduce_scatter x2, waiting for transfers between devices, local(): lax.psum_scatter(terms[4], 'seq', scatter_dimension=0, tiled=True)  279 us
    all_gather x2, waiting for transfers between devices, fetch_forward(): logits = lax.all_gather(mixing[which], 'seq', axis=1, tiled=True)  178 us
    all_gather x2, waiting for transfers between devices, fetch_forward(): lax.all_gather(stacked[4][which], ('seq', 'pos'), axis=0, tiled=True)  128 us
    all_gather x2, waiting for transfers between devices, fetch_forward(): lax.all_gather(stacked[5][which], ('seq', 'pos'), axis=0, tiled=True)  119 us
    reduce_scatter x2, waiting for transfers between devices, local(): lax.psum_scatter(terms[1], 'seq', scatter_dimension=0, tiled=True)  113 us
    unnamed x3, blocking collectives  82.8 us
  transfers between devices with their start and end apart: 31, of which 26 were waited for; matrix products, arithmetic and copies ran while one was open for 14% of the time, Pallas kernels for 0%

commit v1 on v0

v1 whole, which is shorter than its diff:
```python
import jax
import jax.numpy as jnp
from jax import lax
from jax.sharding import PartitionSpec as P

epsilon = 1e-05
both = ("seq", "pos")
bf16 = jnp.bfloat16
f32 = jnp.float32


def dot(spec, left, right):
    return jnp.einsum(spec, left, right, preferred_element_type=f32)


def rms_forward(values, gain):
    inverse = lax.rsqrt(jnp.mean(values * values, axis=-1, keepdims=True) + epsilon)
    return (values * inverse * gain).astype(bf16)


def rms_backward(values, gain, upstream):
    inverse = lax.rsqrt(jnp.mean(values * values, axis=-1, keepdims=True) + epsilon)
    scaled = values * inverse
    grad_gain = jnp.sum(upstream * scaled, axis=0)
    weighted = upstream * gain
    mean = jnp.mean(weighted * scaled, axis=-1, keepdims=True)
    return inverse * (weighted - scaled * mean), grad_gain


def gelu_parts(values):
    inner = 0.7978845608028654 * (values + 0.044715 * values * values * values)
    bent = jnp.tanh(inner)
    half = 0.5 * (1.0 + bent)
    slope = 0.7978845608028654 * (1.0 + 3.0 * 0.044715 * values * values)
    return values * half, half + 0.5 * values * (1.0 - bent * bent) * slope


def pack_weights(which, prenorm, value_proj, out_proj, ffn_gain, up_proj, down_proj):
    width = value_proj.shape[-1]
    pieces = up_proj.shape[-1] // width
    gains = jnp.concatenate([prenorm[which], ffn_gain[which]])
    gains = jnp.pad(gains[None, :], ((0, 7), (0, width - gains.shape[0])))
    ups = [up_proj[which][:, width * b : width * (b + 1)] for b in range(pieces)]
    return jnp.concatenate([value_proj[which], out_proj[which], *ups, down_proj[which], gains])


def unpack_weights(packed, rows, pieces):
    width = packed.shape[-1]
    value_w = packed[:, :rows].reshape(width, width)
    out_w = packed[:, rows : 2 * rows].reshape(width, width)
    ups = [
        packed[:, (2 + b) * rows : (3 + b) * rows].reshape(width, width) for b in range(pieces)
    ]
    low = (2 + pieces) * rows
    down_w = packed[:, low : low + pieces * rows].reshape(pieces * width, width)
    gains = packed[:, low + pieces * rows].astype(f32)
    gain = gains[:, :rows].reshape(width)
    gain_ffn = gains[:, rows : 2 * rows].reshape(width)
    return value_w, out_w, jnp.concatenate(ups, axis=1), down_w, gain, gain_ffn


def pack_grads(value_g, out_g, up_g, down_g, gain_g, gain_ffn_g, count):
    width = value_g.shape[-1]
    rows = width // count
    pieces = up_g.shape[-1] // width
    ups = [up_g[:, width * b : width * (b + 1)].reshape(count, rows, width) for b in range(pieces)]
    gains = jnp.concatenate(
        [gain_g.reshape(count, rows), gain_ffn_g.reshape(count, rows)], axis=1
    ).astype(bf16)
    gains = jnp.pad(gains[:, None, :], ((0, 0), (0, 7), (0, width - 2 * rows)))
    return jnp.concatenate(
        [
            value_g.reshape(count, rows, width),
            out_g.reshape(count, rows, width),
            *ups,
            down_g.reshape(count, pieces * rows, width),
            gains,
        ],
        axis=1,
    )


def unpack_grads(packed, rows, pieces):
    packed = packed.astype(f32)
    low = (2 + pieces) * rows
    ups = [packed[(2 + b) * rows : (3 + b) * rows] for b in range(pieces)]
    gains = packed[low + pieces * rows]
    return (
        gains[:rows],
        packed[:rows],
        packed[rows : 2 * rows],
        gains[rows : 2 * rows],
        jnp.concatenate(ups, axis=1),
        packed[low : low + pieces * rows],
    )


def local(
    inputs, lengths, prenorm, value_proj, mixing, out_proj, ffn_gain, up_proj, down_proj, cotangent
):
    layers, rows, width = value_proj.shape
    pieces = up_proj.shape[-1] // width
    count = width // rows
    slots_here = inputs.shape[1]
    heads = mixing.shape[1]
    slots = mixing.shape[3]
    head_dim = width // (heads * (slots // slots_here))
    position = lax.axis_index("pos") * slots_here + lax.iota(jnp.int32, slots_here)
    live = (position < lengths[0]).astype(f32)[:, None]
    all_lengths = lax.all_gather(lengths, "seq", axis=0, tiled=True)
    seqs = all_lengths.shape[0]
    mask = (lax.iota(jnp.int32, slots)[None, :] < all_lengths[:, None]).astype(f32)

    state = inputs[0].astype(f32) * live
    fetched = []
    stored = []
    for which in range(layers):
        packed = pack_weights(
            which, prenorm, value_proj, out_proj, ffn_gain, up_proj, down_proj
        )
        gathered = lax.all_gather(packed, both, axis=0)
        fetched.append(unpack_weights(gathered, rows, pieces))
    for which in range(layers):
        value_w, out_w, up_w, down_w, gain, gain_ffn = fetched[which]
        normed = rms_forward(state, gain)
        valued = dot("de,td->et", value_w, normed).astype(bf16)
        values = lax.all_to_all(valued, "pos", split_axis=0, concat_axis=1, tiled=True)
        values = lax.all_gather(values, "seq", axis=0)
        values = values.reshape(seqs, heads, head_dim, slots)
        raised = jnp.exp(mixing[which].astype(f32)).astype(bf16)
        totals = dot("sj,hij->shi", mask.astype(bf16), raised)
        inverse = 1.0 / totals
        mixed = dot("shdj,hij->shdi", values, raised) * inverse[:, :, None, :]
        mixed = mixed.astype(bf16)
        back = mixed.reshape(seqs, heads * head_dim, mixed.shape[-1])
        back = lax.all_to_all(back, "seq", split_axis=0, concat_axis=2, tiled=True)[0]
        back = lax.all_to_all(back, "pos", split_axis=1, concat_axis=0, tiled=True)
        returned = (back.T.astype(f32) * live).astype(bf16)
        middle = state + dot("td,de->te", returned, out_w)
        normed_ffn = rms_forward(middle, gain_ffn)
        pre_act = dot("td,df->tf", normed_ffn, up_w)
        activated = gelu_parts(pre_act)[0].astype(bf16)
        stored.append(
            (state, normed, values, raised, inverse, mixed, returned, middle, normed_ffn, pre_act)
        )
        state = middle + dot("tf,fd->td", activated, down_w)

    upstream = cotangent[0].astype(f32) * live
    outcomes = [None] * layers
    logit_grads = [None] * layers
    for which in reversed(range(layers)):
        value_w, out_w, up_w, down_w, gain, gain_ffn = fetched[which]
        before, normed, values, raised, inverse, mixed, returned, middle, normed_ffn, pre_act = (
            stored[which]
        )
        grad_ffn = upstream.astype(bf16)
        activated, slope = gelu_parts(pre_act)
        grad_down = dot("tf,td->fd", activated.astype(bf16), grad_ffn).astype(bf16)
        grad_pre = (dot("td,fd->tf", grad_ffn, down_w) * slope).astype(bf16)
        grad_up = dot("td,tf->df", normed_ffn, grad_pre).astype(bf16)
        step, grad_gain_ffn = rms_backward(middle, gain_ffn, dot("tf,df->td", grad_pre, up_w))
        grad_middle = upstream + step
        grad_mid = grad_middle.astype(bf16)
        grad_out = dot("td,te->de", returned, grad_mid).astype(bf16)
        grad_mixed = dot("ed,td->et", out_w, grad_mid).astype(bf16)
        sent = lax.all_to_all(grad_mixed, "pos", split_axis=0, concat_axis=1, tiled=True)
        sent = sent[None]
        grads = lax.all_to_all(sent, "seq", split_axis=2, concat_axis=0, tiled=True)
        grads = grads.reshape(mixed.shape).astype(f32)
        row_sums = jnp.sum(grads * mixed.astype(f32), axis=2) * inverse
        scaled = (grads * inverse[:, :, None, :]).astype(bf16)
        table = dot("shdi,shdj->hij", scaled, values)
        table = table - jnp.einsum(
            "shi,sj->hij", row_sums, mask, precision=lax.Precision.HIGHEST
        )
        logit_grads[which] = raised.astype(f32) * table
        partial = (dot("shdi,hij->shdj", scaled, raised) * mask[:, None, None, :]).astype(bf16)
        partial = partial.reshape(seqs, heads * head_dim, slots)
        summed = lax.psum_scatter(partial, "seq", scatter_dimension=0, tiled=True)[0]
        grad_valued = lax.all_to_all(summed, "pos", split_axis=1, concat_axis=0, tiled=True)
        grad_value = dot("td,et->de", normed, grad_valued).astype(bf16)
        step, grad_gain = rms_backward(before, gain, dot("et,de->td", grad_valued, value_w))
        upstream = grad_middle + step
        packed = pack_grads(
            grad_value, grad_out, grad_up, grad_down, grad_gain, grad_gain_ffn, count
        )
        reduced = lax.psum_scatter(packed, both, scatter_dimension=0, tiled=True)[0]
        outcomes[which] = unpack_grads(reduced, rows, pieces)
    merged = [jnp.stack([terms[member] for terms in outcomes]) for member in range(6)]
    return (
        state.astype(bf16)[None],
        (upstream * live).astype(bf16)[None],
        merged[0],
        merged[1],
        jnp.stack(logit_grads),
        merged[2],
        merged[3],
        merged[4],
        merged[5],
    )


def solution(mesh):
    return jax.shard_map(
        local,
        mesh=mesh,
        in_specs=(
            P("seq", "pos", None),
            P("seq"),
            P(None, ("seq", "pos")),
            P(None, ("seq", "pos"), None),
            P(None, "pos", "seq", None),
            P(None, ("seq", "pos"), None),
            P(None, ("seq", "pos")),
            P(None, ("seq", "pos"), None),
            P(None, ("seq", "pos"), None),
            P("seq", "pos", None),
        ),
        out_specs=(
            P("seq", "pos", None),
            P("seq", "pos", None),
            P(None, ("seq", "pos")),
            P(None, ("seq", "pos"), None),
            P(None, "pos", "seq", None),
            P(None, ("seq", "pos"), None),
            P(None, ("seq", "pos")),
            P(None, ("seq", "pos"), None),
            P(None, ("seq", "pos"), None),
        ),
        check_vma=False,
    )
```

time: 2300 us -> 1030 us (0.45)
  waiting for transfers between devices: 1770 us -> 670 us
  other arithmetic: 138 us -> 27.1 us
  matrix products: 133 us -> 75.9 us
  blocking collectives: 138 us -> 91.3 us
  local copies, waits for them, and re-layouts: 79 us -> 122 us
    reduce_scatter x18 -> x4, waiting for transfers between devices: 1240 us -> 372 us  [the longest x2 266 us: local(): reduced = lax.psum_scatter(packed, both, scatter_dimension=0, tiled=True)[0]]
    all_gather x10 -> x4, waiting for transfers between devices: 507 us -> 283 us  [the longest x2 181 us: local(): gathered = lax.all_gather(packed, both, axis=0)]
    unnamed x3 -> x1, blocking collectives: 82.8 us -> 10.3 us
    dot_general x30 -> x34, matrix products: 133 us -> 75.9 us  [the longest x32 74.2 us: dot(): return jnp.einsum(spec, left, right, preferred_element_type=f32)]
    reduce_sum x4 -> x3, other arithmetic: 39.9 us -> 1.6 us  [the longest x1 1.24 us: rms_forward(): jnp.mean(values * values, axis=-1, keepdims=True) + epsilon]
    slice x5 -> x18, local copies, waits for them, and re-layouts: 4.99 us -> 34.4 us  [the longest x2 11 us: unpack_weights(): packed[:, (2 + b) * rows:(3 + b) * rows].reshape(width, width)]
    all_to_all x5 -> x7, blocking collectives: 55.1 us -> 81 us  [the longest x2 20.8 us: local(): lax.all_to_all(grad_mixed, 'pos', split_axis=0, concat_axis=1, tiled=True)]
    unnamed x176 -> x226, local copies, waits for them, and re-layouts: 39.7 us -> 49.1 us
  transfers between devices with their start and end apart: 31 -> 13, of which waited for: 26 -> 12; matrix products, arithmetic and copies ran while one was open for 14% -> 10% of each run, Pallas kernels for 0% -> 0%
where the time goes in v1:
time: 1030 us; the launch traced here: 1020 us
  waiting for transfers between devices  670 us (65%)
  local copies, waits for them, and re-layouts  122 us (12%)
  blocking collectives  91.3 us (9%)
  matrix products  75.9 us (7%)
  other arithmetic  27.1 us (3%)
  starting transfers between devices  18.7 us (2%)
  between operations  16.6 us (2%)
    reduce_scatter x2, waiting for transfers between devices, local(): reduced = lax.psum_scatter(packed, both, scatter_dimension=0, tiled=True)[0]  266 us
    all_gather x2, waiting for transfers between devices, local(): gathered = lax.all_gather(packed, both, axis=0)  181 us
    reduce_scatter x2, waiting for transfers between devices, local(): lax.psum_scatter(partial, 'seq', scatter_dimension=0, tiled=True)[0]  106 us
    all_gather x2, waiting for transfers between devices, local(): values = lax.all_gather(values, 'seq', axis=0)  102 us
    dot_general x32, matrix products, dot(): return jnp.einsum(spec, left, right, preferred_element_type=f32)  74.2 us
    unnamed x226, local copies, waits for them, and re-layouts  49.1 us
    all_to_all x2, blocking collectives, local(): lax.all_to_all(grad_mixed, 'pos', split_axis=0, concat_axis=1, tiled=True)  20.8 us
  transfers between devices with their start and end apart: 13, of which 12 were waited for; matrix products, arithmetic and copies ran while one was open for 10% of the time, Pallas kernels for 0%

profile of v1, /device:TPU:0, one launch (start us, length us, event | category | flops | bytes accessed | tf_op | source)
XLA Modules:
  0.0 1022.3 jit_solution(9013513960026489555)
XLA Ops:
  19.3 94.4 %all-gather.11.cloned.1.call-done = bf16[7936,768]{1,0:T(8,128)(2,1)} async-done(((bf16[248,768]{1,0:T(8,128)(2,1)}), bf16[7936,768]{1,0:T(8,128)(2,1)}) %all-gather.11.cloned.1.call-update) | async-done | bytes 12189712 | tf_op jit(solution)/shard_map/all_gather | solution.py:121
  113.7 5.7 fusion.122
  122.3 10.0 all_to_all.176
  137.0 10.3 %all-reduce.4 = s32[8]{0:T(128)S(1)} all-reduce(s32[8]{0:T(128)S(1)} %dynamic-update-slice), channel_id=1, replica_groups=mesh['seq'=8,'pos'=4] {'seq'}, use_global_device_ids=true, to_apply=%add.4 | all-reduce | flops 8 | bytes 64
  147.6 44.6 %all-gather.7.cloned.1.call-done = bf16[8,192,1024]{2,1,0:T(8,128)(2,1)} async-done(((bf16[1,192,1024]{2,1,0:T(8,128)(2,1)}), bf16[8,192,1024]{2,1,0:T(8,128)(2,1)}) %all-gather.7.cloned.1.call-update) | async-done | bytes 3145744 | tf_op jit(solution)/shard_map/all_gather | solution.py:128
  204.3 86.5 %all-gather.13.cloned.1.call-done = bf16[7936,768]{1,0:T(8,128)(2,1)} async-done(((bf16[248,768]{1,0:T(8,128)(2,1)}), bf16[7936,768]{1,0:T(8,128)(2,1)}) %all-gather.13.cloned.1.call-update) | async-done | bytes 12189712 | tf_op jit(solution)/shard_map/all_gather | solution.py:121
  297.5 5.3 fusion.121
  313.3 10.0 all_to_all.177
  327.8 57.3 %all-gather.9.cloned.1.call-done = bf16[8,192,1024]{2,1,0:T(8,128)(2,1)} async-done(((bf16[1,192,1024]{2,1,0:T(8,128)(2,1)}), bf16[8,192,1024]{2,1,0:T(8,128)(2,1)}) %all-gather.9.cloned.1.call-update) | async-done | bytes 3145744 | tf_op jit(solution)/shard_map/all_gather | solution.py:128
  389.0 14.9 %all_to_all.178 = bf16[8,192,128]{2,1,0:T(8,128)(2,1)S(1)} all-to-all(bf16[8,192,128]{2,1,0:T(8,128)(2,1)S(1)} %bitcast.372), channel_id=1, replica_groups=mesh['seq'=8,'pos'=4] {'seq'}, dimensions={0} | all-to-all | bytes 786432 | tf_op jit(solution)/shard_map/all_to_all | solution.py:136
  411.1 4.9 slice.353
  431.8 10.9 %all_to_all.179 = bf16[4,192,256]{2,1,0:T(8,128)(2,1)} all-to-all(bf16[4,192,256]{2,1,0:T(8,128)(2,1)S(1)} %bitcast.368), channel_id=1, replica_groups=mesh['seq'=8,'pos'=4] {'pos'}, dimensions={0} | all-to-all | bytes 786432 | tf_op jit(solution)/shard_map/all_to_all | solution.py:166
  456.4 10.8 %all-to-all-done.7 = bf16[8,2,12288]{2,1,0:T(2,128)(2,1)S(1)} async-done(((bf16[8,2,12288]{2,1,0:T(2,128)(2,1)}), bf16[8,2,12288]{2,1,0:T(2,128)(2,1)S(1)}, u32[]{:S(2)}, u32[]{:S(2)}) %all-to-all-start.7) | async-done | bytes 393248 | tf_op jit(solution)/shard_map/all_to_all | solution.py:168
  476.9 72.8 %reduce-scatter.5.cloned.1.call-done = bf16[1,192,1024]{2,1,0:T(8,128)(2,1)} async-done(((bf16[8,192,1024]{2,1,0:T(8,128)(2,1)}), bf16[1,192,1024]{2,1,0:T(8,128)(2,1)}) %reduce-scatter.5.cloned.1.call-update) | async-done | bytes 393232 | tf_op jit(solution)/shard_map/reduce_scatter | solution.py:179
  552.8 9.9 all_to_all.180
  565.8 5.1 fusion.1
  574.9 10.0 all_to_all.181
  595.7 15.4 %all_to_all.182 = bf16[8,2,12288]{2,1,0:T(2,128)(2,1)} all-to-all(bf16[8,2,12288]{2,1,0:T(2,128)(2,1)S(1)} %reshape.472), channel_id=1, replica_groups=mesh['seq'=8,'pos'=4] {'seq'}, dimensions={0} | all-to-all | bytes 786432 | tf_op jit(solution)/shard_map/all_to_all | solution.py:168
  649.5 5.2 convolution_convert_fusion.3
  659.0 33.4 %reduce-scatter.7.cloned.1.call-done = bf16[1,192,1024]{2,1,0:T(8,128)(2,1)} async-done(((bf16[8,192,1024]{2,1,0:T(8,128)(2,1)}), bf16[1,192,1024]{2,1,0:T(8,128)(2,1)}) %reduce-scatter.7.cloned.1.call-update) | async-done | bytes 393232 | tf_op jit(solution)/shard_map/reduce_scatter | solution.py:179
  718.5 5.0 constant_dynamic-update-slice_fusion.14
  725.5 6.5 fusion.51
  739.8 110.9 %reduce-scatter.11.cloned.1.call-done = bf16[1,248,768]{2,1,0:T(8,128)(2,1)} async-done(((bf16[32,248,768]{2,1,0:T(8,128)(2,1)}), bf16[1,248,768]{2,1,0:T(8,128)(2,1)}) %reduce-scatter.11.cloned.1.call-update) | async-done | bytes 380944 | tf_op jit(solution)/shard_map/reduce_scatter | solution.py:187
  853.6 155.1 %reduce-scatter.9.cloned.1.call-done = bf16[1,248,768]{2,1,0:T(8,128)(2,1)} async-done(((bf16[32,248,768]{2,1,0:T(8,128)(2,1)}), bf16[1,248,768]{2,1,0:T(8,128)(2,1)}) %reduce-scatter.9.cloned.1.call-update) | async-done | bytes 380944 | tf_op jit(solution)/shard_map/reduce_scatter | solution.py:187
  (376 shorter events, 210.9 us)
Async XLA Ops:
  7.2 106.5 %all-gather.11.cloned.1.call-start = ((), (), s32[]{:S(2)}) async-start(), calls=%async_computation.22 | async-start | bytes 12570624 | tf_op jit(solution)/shard_map/all_gather | solution.py:121
  17.3 174.9 %all-gather.7.cloned.1.call-start = ((), (), s32[]{:S(2)}) async-start(), calls=%async_computation.16 | async-start | bytes 3538944 | tf_op jit(solution)/shard_map/all_gather | solution.py:128
  18.0 286.8 %copy-start.69 = (f32[256]{0:T(256)}, f32[256]{0:T(256)S(1)}, u32[]{:S(2)}) copy-start(f32[256]{0:T(256)S(1)} %compare_convert_fusion) | copy-start | bytes 3076
  19.3 102.3 %copy-start.80 = (f32[256]{0:T(256)}, f32[256]{0:T(256)S(1)}, u32[]{:S(2)}) copy-start(f32[256]{0:T(256)S(1)} %add_rsqrt_fusion.3) | copy-start | bytes 3076
  119.3 28.0 %copy-start.5 = (bf16[2,3,128,1024]{3,2,1,0:T(8,128)(2,1)S(1)}, bf16[2,3,128,1024]{3,2,1,0:T(8,128)(2,1)}, u32[]{:S(2)}) copy-start(bf16[2,3,128,1024]{3,2,1,0:T(8,128)(2,1)} %param.14) | copy-start | bytes 4718596
  121.6 26.0 %copy-start.71 = (f32[768]{0:T(1024)}, f32[768]{0:T(1024)S(1)}, u32[]{:S(2)}) copy-start(f32[768]{0:T(1024)S(1)} %mul.432) | copy-start | bytes 9220
  133.6 157.2 %all-gather.13.cloned.1.call-start = ((), (), s32[]{:S(2)}) async-start(), calls=%async_computation.23 | async-start | bytes 12570624 | tf_op jit(solution)/shard_map/all_gather | solution.py:121
  147.3 47.8 %copy-start.82 = (s32[8]{0:T(128)}, s32[8]{0:T(128)S(1)}, u32[]{:S(2)}) copy-start(s32[8]{0:T(128)S(1)} %all-reduce.4) | copy-start | bytes 100
  147.6 47.5 %copy-start.60 = (f32[8,3,128]{2,0,1:T(8,128)}, f32[8,3,128]{2,0,1:T(8,128)S(1)}, u32[]{:S(2)}) copy-start(f32[8,3,128]{2,0,1:T(8,128)S(1)} %convolution_divide_fusion.1) | copy-start | bytes 36868
  196.0 96.7 %all-to-all-start.1 = ((bf16[8,192,128]{2,1,0:T(8,128)(2,1)}), bf16[8,192,128]{2,1,0:T(8,128)(2,1)S(1)}, u32[]{:S(2)}, u32[]{:S(2)}) async-start(bf16[8,192,128]{2,1,0:T(8,128)(2,1)} %bitcast.22), calls=%async_computation.1 | async-start | bytes 786432 | tf_op jit(solution)/shard_map/all_to_all | solution.py:136
  293.9 10.8 %all-to-all-start.2 = ((bf16[192,4,256]{2,0,1:T(8,128)(2,1)}), bf16[192,4,256]{2,0,1:T(8,128)(2,1)S(1)}, u32[]{:S(2)}, u32[]{:S(2)}) async-start(bf16[192,4,256]{2,0,1:T(8,128)(2,1)} %copy.112), calls=%async_computation.2 | async-start | bytes 786432 | tf_op jit(solution)/shard_map/all_to_all | solution.py:137
  297.4 87.7 %all-gather.9.cloned.1.call-start = ((), (), s32[]{:S(2)}) async-start(), calls=%async_computation.17 | async-start | bytes 3538944 | tf_op jit(solution)/shard_map/all_gather | solution.py:128
  302.8 117.0 %copy-start.1 = (bf16[32,24,768]{2,1,0:T(8,128)(2,1)}, bf16[32,24,768]{2,1,0:T(8,128)(2,1)S(1)}, u32[]{:S(2)}) copy-start(bf16[32,24,768]{2,1,0:T(8,128)(2,1)S(1)} %get-tuple-element.21) | copy-start | bytes 3538948
  327.8 60.4 %copy-start.63 = (f32[8,3,128]{2,0,1:T(8,128)}, f32[8,3,128]{2,0,1:T(8,128)S(1)}, u32[]{:S(2)}) copy-start(f32[8,3,128]{2,0,1:T(8,128)S(1)} %convolution_divide_fusion) | copy-start | bytes 36868
  406.9 11.6 %all-to-all-start.5 = ((bf16[192,4,256]{2,0,1:T(8,128)(2,1)}), bf16[192,4,256]{2,0,1:T(8,128)(2,1)}, u32[]{:S(2)}, u32[]{:S(2)}) async-start(bf16[192,4,256]{2,0,1:T(8,128)(2,1)} %copy.118), calls=%async_computation.5 | async-start | bytes 786432 | tf_op jit(solution)/shard_map/all_to_all | solution.py:137
  431.3 133.6 %copy-start = (f32[256,768]{1,0:T(8,128)}, f32[256,768]{1,0:T(8,128)S(1)}, u32[]{:S(2)}) copy-start(f32[256,768]{1,0:T(8,128)S(1)} %fusion.75) | copy-start | bytes 2359300
  431.8 24.0 %copy-start.83 = (s32[8]{0:T(128)S(1)}, s32[8]{0:T(128)}, u32[]{:S(2)}) copy-start(s32[8]{0:T(128)} %copy-done.82) | copy-start | bytes 100
  452.2 15.0 %all-to-all-start.7 = ((bf16[8,2,12288]{2,1,0:T(2,128)(2,1)}), bf16[8,2,12288]{2,1,0:T(2,128)(2,1)S(1)}, u32[]{:S(2)}, u32[]{:S(2)}) async-start(bf16[8,2,12288]{2,1,0:T(2,128)(2,1)} %reshape.470), calls=%async_computation.7 | async-start | bytes 786432 | tf_op jit(solution)/shard_map/all_to_all | solution.py:168
  455.7 94.0 %reduce-scatter.5.cloned.1.call-start = ((), (), s32[]{:S(2)}) async-start(), calls=%async_computation.18 | async-start | bytes 3538944 | tf_op jit(solution)/shard_map/reduce_scatter | solution.py:179
  476.8 85.9 %copy-start.66 = (f32[768]{0:T(1024)S(1)}, f32[768]{0:T(1024)}, u32[]{:S(2)}) copy-start(f32[768]{0:T(1024)} %copy-done.65) | copy-start | bytes 9220
  476.8 215.6 %reduce-scatter.7.cloned.1.call-start = ((), (), s32[]{:S(2)}) async-start(), calls=%async_computation.19 | async-start | bytes 3538944 | tf_op jit(solution)/shard_map/reduce_scatter | solution.py:179
  619.9 230.8 %reduce-scatter.11.cloned.1.call-start = ((), (), s32[]{:S(2)}) async-start(), calls=%async_computation.21 | async-start | bytes 12570624 | tf_op jit(solution)/shard_map/reduce_scatter | solution.py:187
  694.5 10.8 %all-to-all-start.11 = ((bf16[192,4,256]{2,0,1:T(8,128)(2,1)}), bf16[192,4,256]{2,0,1:T(8,128)(2,1)S(1)}, u32[]{:S(2)}, u32[]{:S(2)}) async-start(bf16[192,4,256]{2,0,1:T(8,128)(2,1)} %copy.132), calls=%async_computation.13 | async-start | bytes 786432 | tf_op jit(solution)/shard_map/all_to_all | solution.py:180
  698.0 310.7 %reduce-scatter.9.cloned.1.call-start = ((), (), s32[]{:S(2)}) async-start(), calls=%async_computation.20 | async-start | bytes 12570624 | tf_op jit(solution)/shard_map/reduce_scatter | solution.py:187
  (84 other events, 382.3 us)
Sparse Core Ops, SparseCore 0:
  17.4 96.1 all-gather.10
  133.7 58.4 all-gather.6
  195.7 95.0 all-gather.12
  326.5 58.5 all-gather.8
  476.9 72.7 reduce-scatter.4
  620.0 72.4 reduce-scatter.6
  698.5 152.0 reduce-scatter.10
  856.7 151.9 reduce-scatter.8

commit v2 on v1

--- a/solution.py
+++ b/solution.py
@@ -1,12 +1,737 @@
+import functools
 import jax
 import jax.numpy as jnp
 from jax import lax
+from jax.experimental import pallas as pl
+from jax.experimental.pallas import tpu as pltpu
 from jax.sharding import PartitionSpec as P
 
 epsilon = 1e-05
 both = ("seq", "pos")
 bf16 = jnp.bfloat16
 f32 = jnp.float32
+MESH = pl.DeviceIdType.MESH
+
+
+def own_place():
+    seq = lax.axis_index("seq")
+    pos = lax.axis_index("pos")
+    z = lax.div(seq, 2)
+    y = lax.div(pos, 2)
+    return z, seq - 2 * z, y, pos - 2 * y
+
+
+def device_of(place):
+    z, x, y, c = place
+    return (2 * z + x, 2 * y + c)
+
+
+def order_of(place):
+    z, x, y, c = place
+    return 4 * (2 * z + x) + 2 * y + c
+
+
+def across(place, axis):
+    z, x, y, c = place
+    if axis == "x":
+        return z, 1 - x, y, c
+    if axis == "y":
+        return z, x, 1 - y, c
+    if axis == "xy":
+        return z, 1 - x, 1 - y, c
+    if axis == "core":
+        return z, x, y, 1 - c
+    if axis == "first":
+        return z, x + (1 - c) * (1 - 2 * x), y + c * (1 - 2 * y), c
+    if axis == "second":
+        return z, x + c * (1 - 2 * x), y + (1 - c) * (1 - 2 * y), c
+    if axis == "up":
+        return z + 1, x, y, c
+    return z - 1, x, y, c
+
+
+def shifted(place, step):
+    z, x, y, c = place
+    return z + step, x, y, c
+
+
+def greet(place, axes):
+    barrier = pltpu.get_barrier_semaphore()
+    z = place[0]
+
+    def tell(axis):
+        pl.semaphore_signal(
+            barrier, inc=1, device_id=device_of(across(place, axis)), device_id_type=MESH
+        )
+
+    for axis in axes:
+        tell(axis)
+    pl.when(z < 3)(lambda: tell("up"))
+    pl.when(z > 0)(lambda: tell("down"))
+    ends = jnp.where(z == 0, 1, 0) + jnp.where(z == 3, 1, 0)
+    pl.semaphore_wait(barrier, len(axes) + 2 - ends)
+
+
+class Flow:
+    def __init__(self, place, send, recv):
+        self.place = place
+        self.send = send
+        self.recv = recv
+        self.sent = []
+
+    def push(self, kind, axis, source, target, name, when=None):
+        there = device_of(across(self.place, axis))
+
+        def go(act):
+            copy = pltpu.make_async_remote_copy(
+                src_ref=source,
+                dst_ref=target,
+                send_sem=self.send.at[kind, name],
+                recv_sem=self.recv.at[name],
+                device_id=there,
+                device_id_type=MESH,
+            )
+            act(copy)
+
+        def guarded(act):
+            if when is None:
+                go(act)
+            else:
+                pl.when(when)(lambda: go(act))
+
+        guarded(lambda copy: copy.start())
+        self.sent.append(guarded)
+
+    def arrived(self, target, name):
+        pltpu.make_async_remote_copy(
+            src_ref=target,
+            dst_ref=target,
+            send_sem=self.send.at[0, name],
+            recv_sem=self.recv.at[name],
+            device_id=device_of(across(self.place, "core")),
+            device_id_type=MESH,
+        ).wait_recv()
+
+    def finish(self):
+        for guarded in self.sent:
+            guarded(lambda copy: copy.wait_send())
+
+
+UP, DOWN, FIRST, SECOND, CORE = range(5)
+
+
+class WeightGather(Flow):
+    def __init__(self, place, own, out, send, recv):
+        super().__init__(place, send, recv)
+        self.own = own
+        self.out = out
+
+    def spread(self, origin, source, line=None, second=True, first=True, when=None):
+        name = order_of(origin)
+        target = self.out.at[name]
+        z = self.place[0]
+        for kind, axis, guard in ((UP, "up", z < 3), (DOWN, "down", z > 0)):
+            if line is not None and axis in line:
+                both = guard if when is None else guard & when
+                self.push(kind, axis, source, target, name, both)
+        if second:
+            self.push(SECOND, "second", source, target, name, when)
+        if first:
+            self.push(FIRST, "first", source, target, name, when)
+        self.push(CORE, "core", source, target, name, when)
+
+    def begin(self):
+        self.spread(self.place, self.own, line=("up", "down"))
+
+    def line_step(self, step):
+        z = self.place[0]
+        for sign, line in ((-1, "up"), (1, "down")):
+            origin = shifted(self.place, sign * step)
+            valid = (origin[0] >= 0) & (origin[0] <= 3)
+            name = order_of(origin)
+            pl.when(valid)(lambda n=name: self.arrived(self.out.at[n], n))
+            self.spread(origin, self.out.at[name], line=(line,), when=valid)
+
+    def each(self, base, step):
+        if step == 0:
+            yield base, None
+            return
+        for sign in (-1, 1):
+            origin = shifted(base, sign * step)
+            yield origin, (origin[0] >= 0) & (origin[0] <= 3)
+
+    def take(self, axis, step, first):
+        base = across(self.place, axis)
+        for origin, valid in self.each(base, step):
+            name = order_of(origin)
+            target = self.out.at[name]
+            if valid is None:
+                self.arrived(target, name)
+            else:
+                pl.when(valid)(lambda t=target, n=name: self.arrived(t, n))
+            if first:
+                self.push(FIRST, "first", target, target, name, valid)
+            self.push(CORE, "core", target, target, name, valid)
+
+    def second_step(self, step):
+        self.take("second", step, True)
+
+    def first_step(self, step):
+        self.take("first", step, False)
+        base = across(across(self.place, "first"), "second")
+        for origin, valid in self.each(base, step):
+            name = order_of(origin)
+            target = self.out.at[name]
+            if valid is None:
+                self.arrived(target, name)
+            else:
+                pl.when(valid)(lambda t=target, n=name: self.arrived(t, n))
+            self.push(CORE, "core", target, target, name, valid)
+
+    def end(self):
+        z, x, y, c = self.place
+        for q in range(8):
+            for yy in range(2):
+                name = 4 * q + 2 * yy + 1 - c
+                self.arrived(self.out.at[name], name)
+
+
+class ValueGather(Flow):
+    def __init__(self, place, blocks, out, send, recv):
+        super().__init__(place, send, recv)
+        self.blocks = blocks
+        self.out = out
+
+    def spot(self, origin):
+        z, x, y, c = origin
+        rows = self.blocks.shape[2]
+        columns = self.blocks.shape[3]
+        return self.out.at[
+            :,
+            pl.ds(pl.multiple_of((2 * z + x) * rows, rows), rows),
+            pl.ds(pl.multiple_of((2 * y + c) * columns, columns), columns),
+        ]
+
+    def begin(self):
+        z, x, y, c = self.place
+        spot = self.spot(self.place)
+        name = order_of(self.place)
+        for kind, axis in enumerate(("xy", "x", "y")):
+            there = across(self.place, axis)
+            self.push(UP + kind, axis, self.blocks.at[2 * there[2] + there[1]], spot, name)
+        mine = self.blocks.at[2 * y + x]
+        self.relay(self.place, mine, ("up", "down"), kinds=(3, 4, 5))
+
+    def keep(self, sem):
+        z, x, y, c = self.place
+        return pltpu.make_async_copy(self.blocks.at[2 * y + x], self.spot(self.place), sem)
+
+    def relay(self, origin, source, line, when=None, kinds=(UP, DOWN, 2)):
+        z = self.place[0]
+        name = order_of(origin)
+        target = self.spot(origin)
+        for kind, axis, guard in ((kinds[0], "up", z < 3), (kinds[1], "down", z > 0)):
+            if axis in line:
+                both = guard if when is None else guard & when
+                self.push(kind, axis, source, target, name, both)
+        self.push(kinds[2], "core", source, target, name, when)
+
+    def plane(self):
+        for axis in ("x", "y", "xy"):
+            origin = across(self.place, axis)
+            spot = self.spot(origin)
+            self.arrived(spot, order_of(origin))
+            self.relay(origin, spot, ("up", "down"))
+
+    def line_step(self, step):
+        for sign, line in ((-1, "up"), (1, "down")):
+            base = shifted(self.place, sign * step)
+            valid = (base[0] >= 0) & (base[0] <= 3)
+            for axis in ("", "x", "y", "xy"):
+                origin = base if axis == "" else across(base, axis)
+                spot = self.spot(origin)
+                name = order_of(origin)
+                pl.when(valid)(lambda s=spot, n=name: self.arrived(s, n))
+                self.relay(origin, spot, (line,), when=valid)
+
+    def end(self):
+        z, x, y, c = self.place
+        for q in range(8):
+            for yy in range(2):
+                origin = (q // 2, q % 2, yy, 1 - c)
+                self.arrived(self.spot(origin), order_of(origin))
+
+
+def gather_kernel(with_values, own, *refs):
+    place = own_place()
+    if with_values:
+        blocks, out, values, send_w, recv_w, send_v, recv_v, local = refs
+        value_flow = ValueGather(place, blocks, values, send_v, recv_v)
+        kept = value_flow.keep(local.at[1])
+    else:
+        out, send_w, recv_w, local = refs
+    weight_flow = WeightGather(place, own, out, send_w, recv_w)
+    stay = pltpu.make_async_copy(own, out.at[order_of(place)], local.at[0])
+    stay.start()
+    if with_values:
+        kept.start()
+    greet(place, ("x", "y", "core") + (("xy",) if with_values else ()))
+    weight_flow.begin()
+    if with_values:
+        value_flow.begin()
+        value_flow.plane()
+    weight_flow.line_step(1)
+    if with_values:
+        value_flow.line_step(1)
+    weight_flow.second_step(0)
+    weight_flow.line_step(2)
+    if with_values:
+        value_flow.line_step(2)
+    weight_flow.second_step(1)
+    weight_flow.first_step(0)
+    weight_flow.line_step(3)
+    weight_flow.second_step(2)
+    weight_flow.first_step(1)
+    if with_values:
+        value_flow.line_step(3)
+    weight_flow.second_step(3)
+    weight_flow.first_step(2)
+    weight_flow.first_step(3)
+    if with_values:
+        value_flow.end()
+    weight_flow.end()
+    stay.wait()
+    if with_values:
+        kept.wait()
+        value_flow.finish()
+    weight_flow.finish()
+
+
+def gather(packed, blocks, collective_id):
+    anywhere = pl.BlockSpec(memory_space=pl.ANY)
+    with_values = blocks is not None
+    out_shape = [jax.ShapeDtypeStruct((32,) + packed.shape, packed.dtype)]
+    scratch = [pltpu.SemaphoreType.DMA((5, 32)), pltpu.SemaphoreType.DMA((32,))]
+    operands = [packed]
+    if with_values:
+        groups, heads, size, columns = blocks.shape
+        out_shape.append(jax.ShapeDtypeStruct((heads, 8 * size, 4 * columns), blocks.dtype))
+        scratch += [pltpu.SemaphoreType.DMA((6, 32)), pltpu.SemaphoreType.DMA((32,))]
+        operands.append(blocks)
+    scratch.append(pltpu.SemaphoreType.DMA((2,)))
+    return pl.pallas_call(
+        functools.partial(gather_kernel, with_values),
+        out_shape=out_shape,
+        in_specs=[anywhere] * len(operands),
+        out_specs=[anywhere] * len(out_shape),
+        scratch_shapes=scratch,
+        compiler_params=pltpu.CompilerParams(collective_id=collective_id, has_side_effects=True),
+    )(*operands)
+
+
+def line_order(z):
+    high = lax.div(z, 2)
+    return (3 - 3 * high, 2 - high, 1 - z + 4 * high, z)
+
+
+def slot_of(place):
+    z, x, y, c = place
+    return 4 * z + 2 * x + y
+
+
+class Reduce(Flow):
+    def load(self, source, slot):
+        return pltpu.make_async_copy(source, self.mine.at[slot], self.loaded.at[slot])
+
+    def wait_slot(self, buffer, kind, slot):
+        pltpu.make_async_remote_copy(
+            src_ref=buffer.at[slot],
+            dst_ref=buffer.at[slot],
+            send_sem=self.send.at[kind, slot],
+            recv_sem=self.recv.at[kind, slot],
+            device_id=device_of(across(self.place, "core")),
+            device_id_type=MESH,
+        ).wait_recv()
+
+    def push_slot(self, kind, axis, source, target, slot, when=None):
+        there = device_of(across(self.place, axis))
+
+        def guarded(act):
+            def go():
+                act(
+                    pltpu.make_async_remote_copy(
+                        src_ref=source,
+                        dst_ref=target,
+                        send_sem=self.send.at[kind, slot],
+                        recv_sem=self.recv.at[kind, slot],
+                        device_id=there,
+                        device_id_type=MESH,
+                    )
+                )
+
+            if when is None:
+                go()
+            else:
+                pl.when(when)(go)
+
+        guarded(lambda copy: copy.start())
+        self.sent.append(guarded)
+
+    def total(self, slot, buffers, out=None):
+        rows = self.mine.shape[1]
+        step = self.step
+
+        def body(j, carry):
+            part = pl.ds(pl.multiple_of(j * step, step), step)
+            value = self.mine[slot, part].astype(f32)
+            for buffer in buffers:
+                value = value + buffer[slot, part].astype(f32)
+            if out is None:
+                self.mine[slot, part] = value.astype(self.mine.dtype)
+            else:
+                out[part] = value.astype(out.dtype)
+            return carry
+
+        lax.fori_loop(0, rows // step, body, 0)
+
+    def line(self, there, slot, buffers, last):
+        z = self.place[0]
+        below, above = self.below, self.above
+
+        @pl.when((there > z) & (z > 0))
+        def _():
+            self.wait_slot(below, 3, slot)
+            self.total(slot, buffers + [below])
+
+        @pl.when((there > z) & (z == 0))
+        def _():
+            self.total(slot, buffers)
+
+        @pl.when((there < z) & (z < 3))
+        def _():
+            self.wait_slot(above, 4, slot)
+            self.total(slot, buffers + [above])
+
+        @pl.when((there < z) & (z == 3))
+        def _():
+            self.total(slot, buffers)
+
+        self.push_slot(3, "up", self.mine.at[slot], below.at[slot], slot, there > z)
+        self.push_slot(4, "down", self.mine.at[slot], above.at[slot], slot, there < z)
+
+    def close(self, slot, buffers, out=None):
+        z = self.place[0]
+
+        @pl.when(z > 0)
+        def _():
+            self.wait_slot(self.below, 3, slot)
+
+        @pl.when(z < 3)
+        def _():
+            self.wait_slot(self.above, 4, slot)
+
+        @pl.when(z == 0)
+        def _():
+            self.total(slot, buffers + [self.above], out)
+
+        @pl.when(z == 3)
+        def _():
+            self.total(slot, buffers + [self.below], out)
+
+        @pl.when((z > 0) & (z < 3))
+        def _():
+            self.total(slot, buffers + [self.below, self.above], out)
+
+
+class WeightReduce(Reduce):
+    def __init__(self, place, packed, out, mine, partner, first, second, below, above, send, recv, loaded):
+        super().__init__(place, send, recv)
+        self.packed, self.out, self.mine, self.partner = packed, out, mine, partner
+        self.first, self.second, self.below, self.above = first, second, below, above
+        self.loaded = loaded
+        rows = mine.shape[1]
+        self.step = next(s for s in (48, 80, 112, 32, 16) if rows % s == 0)
+
+    def group(self, place, which):
+        base = place
+        if which in "AB":
+            base = across(base, "first")
+        if which in "AC":
+            base = across(base, "second")
+        return [(there,) + base[1:] for there in line_order(place[0])]
+
+    def begin(self, which):
+        partner = across(self.place, "core")
+        for goal in self.group(partner, which):
+            slot = slot_of(goal)
+            self.push_slot(
+                0, "core", self.packed.at[order_of(goal)], self.partner.at[slot], slot
+            )
+        for goal in self.group(self.place, which):
+            self.load(self.packed.at[order_of(goal)], slot_of(goal)).start()
+
+    def ready(self, goal, kinds):
+        slot = slot_of(goal)
+        self.load(self.packed.at[order_of(goal)], slot).wait()
+        buffers = [self.partner, self.first, self.second][:kinds]
+        for kind, buffer in enumerate(buffers):
+            self.wait_slot(buffer, kind, slot)
+        return slot, buffers
+
+    def far(self, which):
+        for goal in self.group(self.place, which):
+            slot, buffers = self.ready(goal, 1)
+            self.total(slot, buffers)
+            self.push_slot(1, "first", self.mine.at[slot], self.first.at[slot], slot)
+
+    def near(self):
+        for goal in self.group(self.place, "C"):
+            slot, buffers = self.ready(goal, 2)
+            self.total(slot, buffers)
+            self.push_slot(2, "second", self.mine.at[slot], self.second.at[slot], slot)
+
+    def column(self):
+        goals = self.group(self.place, "D")
+        for goal in goals[:3]:
+            slot, buffers = self.ready(goal, 3)
+            self.line(goal[0], slot, buffers, None)
+        slot, buffers = self.ready(goals[3], 3)
+        self.close(slot, buffers, self.out)
+
+
+class ValueReduce(Reduce):
+    def __init__(self, place, partial, out, mine, partner, below, above, send, recv, loaded, landed, kept):
+        super().__init__(place, send, recv)
+        self.partial, self.out, self.mine, self.partner = partial, out, mine, partner
+        self.below, self.above, self.loaded, self.landed, self.kept = below, above, loaded, landed, kept
+        self.step = mine.shape[1]
+
+    def spot(self, goal):
+        z, x, y, c = goal
+        rows = self.mine.shape[2]
+        columns = self.mine.shape[3]
+        return self.partial.at[
+            :,
+            pl.ds(pl.multiple_of((2 * z + x) * rows, rows), rows),
+            pl.ds(pl.multiple_of((2 * y + c) * columns, columns), columns),
+        ]
+
+    def group(self, place, k):
+        z, x, y, c = place
+        there = line_order(z)[k]
+        return [(there, xx, yy, c) for xx in range(2) for yy in range(2)]
+
+    def begin(self, k):
+        for goal in self.group(across(self.place, "core"), k):
+            slot = slot_of(goal)
+            self.push_slot(0, "core", self.spot(goal), self.partner.at[slot], slot)
+        for goal in self.group(self.place, k):
+            self.load(self.spot(goal), slot_of(goal)).start()
+
+    def ready(self, goal):
+        slot = slot_of(goal)
+        self.load(self.spot(goal), slot).wait()
+        self.wait_slot(self.partner, 0, slot)
+        return slot
+
+    def pass_on(self, k):
+        for goal in self.group(self.place, k):
+            slot = self.ready(goal)
+            self.line(goal[0], slot, [self.partner], None)
+
+    def land(self):
+        z, x, y, c = self.place
+        own = 2 * y + x
+        for axis in ("xy", "x", "y", ""):
+            goal = self.place if axis == "" else across(self.place, axis)
+            slot = self.ready(goal)
+            self.close(slot, [self.partner])
+            if axis == "":
+                self.stay = pltpu.make_async_copy(
+                    self.mine.at[slot], self.out.at[own], self.kept.at[0]
+                )
+                self.stay.start()
+            else:
+                kind = {"xy": 0, "x": 1, "y": 2}[axis]
+                copy = pltpu.make_async_remote_copy(
+                    src_ref=self.mine.at[slot],
+                    dst_ref=self.out.at[own],
+                    send_sem=self.kept.at[1 + kind],
+                    recv_sem=self.landed.at[kind],
+                    device_id=device_of(goal),
+                    device_id_type=MESH,
+                )
+                copy.start()
+                self.sent.append(lambda act, copy=copy: act(copy))
+
+    def end(self):
+        for kind, axis in enumerate(("xy", "x", "y")):
+            z, x, y, c = across(self.place, axis)
+            target = self.out.at[2 * y + x]
+            pltpu.make_async_remote_copy(
+                src_ref=target,
+                dst_ref=target,
+                send_sem=self.kept.at[1 + kind],
+                recv_sem=self.landed.at[kind],
+                device_id=device_of((z, x, y, c)),
+                device_id_type=MESH,
+            ).wait_recv()
+        self.stay.wait()
+
+
+def reduce_kernel(with_values, packed, *refs):
+    place = own_place()
+    if with_values:
+        partial, out, values, *rest = refs
+        wide, rest = rest[:9], rest[9:]
+        value_flow = ValueReduce(place, partial, values, *rest)
+    else:
+        out, *wide = refs
+    weight_flow = WeightReduce(place, packed, out, *wide)
+    greet(place, ("x", "y", "core") + (("xy",) if with_values else ()))
+    for k, which in enumerate("ABCD"):
+        if with_values:
+            value_flow.begin(k)
+        weight_flow.begin(which)
+    weight_flow.far("A")
+    if with_values:
+        value_flow.pass_on(0)
+    weight_flow.far("B")
+    if with_values:
+        value_flow.pass_on(1)
+    weight_flow.near()
+    if with_values:
+        value_flow.pass_on(2)
+    weight_flow.column()
+    if with_values:
+        value_flow.land()
+        value_flow.end()
+        value_flow.finish()
+    weight_flow.finish()
+
+
+def reduce(packed, partial, collective_id):
+    anywhere = pl.BlockSpec(memory_space=pl.ANY)
+    with_values = partial is not None
+    _, rows, width = packed.shape
+    out_shape = [jax.ShapeDtypeStruct((rows, width), f32)]
+    out_specs = [pl.BlockSpec(memory_space=pltpu.VMEM)]
+    dma = pltpu.SemaphoreType.DMA
+    scratch = [pltpu.VMEM((16, rows, width), bf16) for _ in range(6)]
+    scratch += [dma((5, 16)), dma((5, 16)), dma((16,))]
+    operands = [packed]
+    if with_values:
+        heads, tall, long = partial.shape
+        block = (heads, tall // 8, long // 4)
+        out_shape.append(jax.ShapeDtypeStruct((4,) + block, bf16))
+        out_specs.append(anywhere)
+        scratch += [pltpu.VMEM((16,) + block, bf16) for _ in range(4)]
+        scratch += [dma((5, 16)), dma((5, 16)), dma((16,)), dma((3,)), dma((4,))]
+        operands.append(partial)
+    return pl.pallas_call(
+        functools.partial(reduce_kernel, with_values),
+        out_shape=out_shape,
+        in_specs=[anywhere] * len(operands),
+        out_specs=out_specs,
+        scratch_shapes=scratch,
+        compiler_params=pltpu.CompilerParams(
+            collective_id=collective_id, has_side_effects=True, vmem_limit_bytes=60000 * 1024
+        ),
+    )(*operands)
+
+
+def trade_kernel(to_rows, source, out, send, recv, local):
+    place = own_place()
+    z, x, y, c = place
+    seq, pos = 2 * z + x, 2 * y + c
+    width = out.shape[3] if to_rows else source.shape[3]
+
+    def wide(ref, group, half):
+        return ref.at[group, :, :, pl.ds(pl.multiple_of(half * width, width), width)]
+
+    by_items = [((q // 2, q % 2, lax.div(z, 2), z - 2 * lax.div(z, 2)), q) for q in range(8)]
+    by_parts = [((pos, g % 2, g // 2, half), 2 * g + half) for g in range(4) for half in range(2)]
+    goals, origins = (by_parts, by_items) if to_rows else (by_items, by_parts)
+    own_name = seq if to_rows else 2 * (2 * y + x) + c
+
+    def is_own(there):
+        return order_of(there) == order_of(place)
+
+    barrier = pltpu.get_barrier_semaphore()
+    for there, _ in origins:
+
+        @pl.when(jnp.logical_not(is_own(there)))
+        def _(there=there):
+            pl.semaphore_signal(barrier, inc=1, device_id=device_of(there), device_id_type=MESH)
+
+    pl.semaphore_wait(barrier, 8 - jnp.where(pos == z, 1, 0))
+
+    def ends(name):
+        if to_rows:
+            return wide(source, name // 2, name % 2), out.at[:, seq]
+        return source.at[:, name], wide(out, 2 * y + x, c)
+
+    def landing(name):
+        if to_rows:
+            return out.at[:, name]
+        return wide(out, name // 2, name % 2)
+
+    def remote(there, name):
+        begin, end = ends(name)
+        return pltpu.make_async_remote_copy(
+            src_ref=begin,
+            dst_ref=end,
+            send_sem=send.at[name],
+            recv_sem=recv.at[own_name],
+            device_id=device_of(there),
+            device_id_type=MESH,
+        )
+
+    def here(name):
+        begin, end = ends(name)
+        return pltpu.make_async_copy(begin, end, local)
+
+    for there, name in goals:
+        own = is_own(there)
+        pl.when(jnp.logical_not(own))(lambda: remote(there, name).start())
+        pl.when(own)(lambda: here(name).start())
+    for there, name in origins:
+        target = landing(name)
+
+        @pl.when(jnp.logical_not(is_own(there)))
+        def _(target=target, name=name, there=there):
+            pltpu.make_async_remote_copy(
+                src_ref=target,
+                dst_ref=target,
+                send_sem=send.at[name],
+                recv_sem=recv.at[name],
+                device_id=device_of(there),
+                device_id_type=MESH,
+            ).wait_recv()
+
+    for there, name in goals:
+        own = is_own(there)
+        pl.when(jnp.logical_not(own))(lambda: remote(there, name).wait_send())
+        pl.when(own)(lambda: here(name).wait())
+
+
+def trade(array, to_rows, collective_id):
+    anywhere = pl.BlockSpec(memory_space=pl.ANY)
+    if to_rows:
+        _, heads, size, positions = array.shape
+        shape = (heads, 8, size, positions // 2)
+    else:
+        heads, _, size, positions = array.shape
+        shape = (4, heads, size, positions * 2)
+    dma = pltpu.SemaphoreType.DMA
+    return pl.pallas_call(
+        functools.partial(trade_kernel, to_rows),
+        out_shape=jax.ShapeDtypeStruct(shape, array.dtype),
+        in_specs=[anywhere],
+        out_specs=anywhere,
+        scratch_shapes=[dma((8,)), dma((8,)), dma],
+        compiler_params=pltpu.CompilerParams(collective_id=collective_id, has_side_effects=True),
+    )(array)
 
 
 def dot(spec, left, right):
@@ -200,9 +925,160 @@
     )
 
 
+def split_columns(matrix, width):
+    return [matrix[:, low : low + width] for low in range(0, matrix.shape[1], width)]
+
+
+def from_slices(packed, low, rows, width):
+    return packed[:, low : low + rows].reshape(-1, width)
+
+
+def to_slices(matrix, count):
+    return matrix.reshape(count, -1, matrix.shape[-1])
+
+
+def local_direct(
+    inputs, lengths, prenorm, value_proj, mixing, out_proj, ffn_gain, up_proj, down_proj, cotangent
+):
+    layers, rows, width = value_proj.shape
+    pieces = up_proj.shape[-1] // width
+    count = width // rows
+    slots_here = inputs.shape[1]
+    heads, rows_here, slots = mixing.shape[1:]
+    head_dim = width // (heads * 4)
+    seqs = 8
+    position = lax.axis_index("pos") * slots_here + lax.iota(jnp.int32, slots_here)
+    live = (position < lengths[0]).astype(f32)[:, None]
+    swap = []
+    for seq in range(8):
+        for pos in range(4):
+            there = (seq - seq % 2 + pos % 2, pos - pos % 2 + seq % 2)
+            swap.append((4 * seq + pos, 4 * there[0] + there[1]))
+    logits = lax.ppermute(mixing, both, swap)
+
+    high = lengths // 32
+    small = jnp.concatenate(
+        [prenorm.reshape(-1), ffn_gain.reshape(-1), high.astype(bf16), (lengths - 32 * high).astype(bf16)]
+    )
+    small = jnp.pad(small[None, :], ((0, 7), (0, width - small.shape[0])))
+    (first,) = gather(jnp.concatenate([value_proj[0], small]), None, 0)
+    value_w = [from_slices(first, 0, rows, width), None]
+    small = first[:, rows].astype(f32)
+    gains = small[:, : 4 * rows].reshape(count, 4, rows).transpose(1, 0, 2).reshape(4, width)
+    told = small[:, 4 * rows : 4 * rows + 2]
+    told = (told[:, 0] * 32.0 + told[:, 1]).astype(jnp.int32)
+    all_lengths = told.reshape(seqs, -1)[:, 0]
+    mask = (lax.iota(jnp.int32, slots)[None, :] < all_lengths[:, None]).astype(f32)
+
+    state = inputs[0].astype(f32) * live
+    fetched = []
+    stored = []
+    for which in range(layers):
+        gain, gain_ffn = gains[which], gains[layers + which]
+        normed = rms_forward(state, gain)
+        valued = dot("de,td->et", value_w[which], normed).astype(bf16)
+        valued = valued.reshape(4, heads, head_dim, slots_here)
+        packed = [out_proj[which], *split_columns(up_proj[which], width), down_proj[which]]
+        if which + 1 < layers:
+            packed.append(value_proj[which + 1])
+        gathered, values = gather(jnp.concatenate(packed), valued, 1 + which)
+        out_w = from_slices(gathered, 0, rows, width)
+        ups = [from_slices(gathered, (1 + b) * rows, rows, width) for b in range(pieces)]
+        up_w = jnp.concatenate(ups, axis=1)
+        down_w = from_slices(gathered, (1 + pieces) * rows, pieces * rows, width)
+        if which + 1 < layers:
+            value_w[which + 1] = from_slices(gathered, (1 + 2 * pieces) * rows, rows, width)
+        fetched.append((out_w, up_w, down_w))
+        raised = jnp.exp(logits[which].astype(f32)).astype(bf16)
+        totals = dot("sj,hij->hsi", mask.astype(bf16), raised)
+        inverse = 1.0 / totals
+        mixed = dot("hsj,hij->hsi", values, raised).reshape(heads, seqs, head_dim, rows_here)
+        mixed = (mixed * inverse[:, :, None, :]).astype(bf16)
+        returned = trade(mixed, False, 3 + which).reshape(width, slots_here)
+        returned = (returned.astype(f32) * live[:, 0]).astype(bf16)
+        middle = state + dot("dt,de->te", returned, out_w)
+        normed_ffn = rms_forward(middle, gain_ffn)
+        pre_act = dot("td,df->tf", normed_ffn, up_w)
+        activated = gelu_parts(pre_act)[0].astype(bf16)
+        stored.append(
+            (state, normed, values, raised, inverse, mixed, returned, middle, normed_ffn, pre_act)
+        )
+        state = middle + dot("tf,fd->td", activated, down_w)
+
+    upstream = cotangent[0].astype(f32) * live
+    value_g, gain_g, reduced, logit_g = [None] * layers, [None] * layers, [None] * layers, [None] * layers
+    for which in reversed(range(layers)):
+        gain, gain_ffn = gains[which], gains[layers + which]
+        out_w, up_w, down_w = fetched[which]
+        before, normed, values, raised, inverse, mixed, returned, middle, normed_ffn, pre_act = (
+            stored[which]
+        )
+        grad_ffn = upstream.astype(bf16)
+        activated, slope = gelu_parts(pre_act)
+        grad_down = dot("tf,td->fd", activated.astype(bf16), grad_ffn).astype(bf16)
+        grad_pre = (dot("td,fd->tf", grad_ffn, down_w) * slope).astype(bf16)
+        grad_up = dot("td,tf->df", normed_ffn, grad_pre).astype(bf16)
+        step, grad_gain_ffn = rms_backward(middle, gain_ffn, dot("tf,df->td", grad_pre, up_w))
+        grad_middle = upstream + step
+        grad_mid = grad_middle.astype(bf16)
+        grad_out = dot("dt,te->de", returned, grad_mid).astype(bf16)
+        grad_mixed = dot("ed,td->et", out_w, grad_mid).astype(bf16)
+        grads = trade(grad_mixed.reshape(4, heads, head_dim, slots_here), True, 5 + which)
+        grads = grads.astype(f32)
+        row_sums = jnp.sum(grads * mixed.astype(f32), axis=2) * inverse
+        scaled = (grads * inverse[:, :, None, :]).astype(bf16)
+        scaled = scaled.reshape(heads, seqs * head_dim, rows_here)
+        partial = dot("hsi,hij->hsj", scaled, raised).reshape(heads, seqs, head_dim, slots)
+        partial = (partial * mask[None, :, None, :]).astype(bf16)
+        packed = [
+            to_slices(grad_out, count),
+            *[to_slices(part, count) for part in split_columns(grad_up, width)],
+            to_slices(grad_down, count),
+        ]
+        if which + 1 < layers:
+            packed.append(to_slices(value_g[which + 1], count))
+        else:
+            packed.append(jnp.zeros((count, 8, width), bf16))
+        partial = partial.reshape(heads, seqs * head_dim, slots)
+        reduced[which], grad_valued = reduce(jnp.concatenate(packed, axis=1), partial, 7 + which)
+        table = dot("hsi,hsj->hij", scaled, values)
+        table = table - jnp.einsum("hsi,sj->hij", row_sums, mask, precision=lax.Precision.HIGHEST)
+        logit_g[which] = lax.ppermute((raised.astype(f32) * table).astype(bf16), both, swap)
+        grad_valued = grad_valued.reshape(width, slots_here)
+        value_g[which] = dot("td,et->de", normed, grad_valued).astype(bf16)
+        step, grad_gain = rms_backward(before, gain, dot("et,de->td", grad_valued, value_w[which]))
+        gain_g[which] = (grad_gain, grad_gain_ffn)
+        upstream = grad_middle + step
+
+    small = jnp.stack([gain_g[0][0], gain_g[1][0], gain_g[0][1], gain_g[1][1]])
+    small = small.reshape(4, count, rows).transpose(1, 0, 2).reshape(count, 1, 4 * rows)
+    small = jnp.pad(small.astype(bf16), ((0, 0), (0, 7), (0, width - 4 * rows)))
+    (last,) = reduce(jnp.concatenate([to_slices(value_g[0], count), small], axis=1), None, 9)
+    small = last[rows, : 4 * rows].reshape(2, layers, rows)
+    low = (1 + 2 * pieces) * rows
+
+    def up_part(packed):
+        return jnp.concatenate(
+            [packed[(1 + b) * rows : (2 + b) * rows] for b in range(pieces)], axis=1
+        )
+
+    return (
+        state.astype(bf16)[None],
+        (upstream * live).astype(bf16)[None],
+        small[0],
+        jnp.stack([last[:rows], reduced[0][low : low + rows]]),
+        jnp.stack(logit_g).astype(f32),
+        jnp.stack([packed[:rows] for packed in reduced]),
+        small[1],
+        jnp.stack([up_part(packed) for packed in reduced]),
+        jnp.stack([packed[(1 + pieces) * rows : low] for packed in reduced]),
+    )
+
+
 def solution(mesh):
+    direct = mesh.shape["seq"] == 8 and mesh.shape["pos"] == 4
     return jax.shard_map(
-        local,
+        local_direct if direct else local,
         mesh=mesh,
         in_specs=(
             P("seq", "pos", None),

time: 1030 us -> 598 us (0.58)
  waiting for transfers between devices: 670 us -> 0.01 us
  Pallas kernels: 0 us -> 418 us
  blocking collectives: 91.3 us -> 0 us
  local copies, waits for them, and re-layouts: 122 us -> 68.8 us
  between operations: 16.6 us -> 2.89 us
  matrix products: 75.9 us -> 65 us
    pallas_call x0 -> x10, Pallas kernels: none -> 418 us  [the longest x3 193 us: reduce(): pl.pallas_call(functools.partial(reduce_kernel, with_values), out_shape=o...]
    reduce_scatter x4 -> x0, waiting for transfers between devices: 372 us -> none  [the longest x2 266 us: local(): reduced = lax.psum_scatter(packed, both, scatter_dimension=0, tiled=True)[0]]
    all_gather x4 -> x0, waiting for transfers between devices: 283 us -> none  [the longest x2 181 us: local(): gathered = lax.all_gather(packed, both, axis=0)]
    all_to_all x7 -> x0, blocking collectives: 81 us -> none  [the longest x2 20.8 us: local(): lax.all_to_all(grad_mixed, 'pos', split_axis=0, concat_axis=1, tiled=True)]
    unnamed x226 -> x189, local copies, waits for them, and re-layouts: 49.1 us -> 24.1 us
    all_to_all x5 -> x0, starting transfers between devices: 17.9 us -> none  [the longest x2 7.58 us: local(): back = lax.all_to_all(back, 'pos', split_axis=1, concat_axis=0, tiled=True)]
    all_to_all x5 -> x0, waiting for transfers between devices: 15.4 us -> none  [the longest x1 10.8 us: local(): grads = lax.all_to_all(sent, 'seq', split_axis=2, concat_axis=0, tiled=True)]
    all_to_all x14 -> x0, local copies, waits for them, and re-layouts: 14.9 us -> none  [the longest x4 5.14 us: local(): lax.all_to_all(summed, 'pos', split_axis=1, concat_axis=0, tiled=True)]
  transfers between devices with their start and end apart: 13 -> 3, of which waited for: 12 -> 0; matrix products, arithmetic and copies ran while one was open for 10% -> 7% of each run, Pallas kernels for 0% -> 18%
where the time goes in v2:
time: 598 us; the launch traced here: 591 us
  Pallas kernels  418 us (70%)
  local copies, waits for them, and re-layouts  68.8 us (12%)
  matrix products  65 us (11%)
  other arithmetic  24.8 us (4%)
  starting transfers between devices  11.5 us (2%)
    pallas_call x3, Pallas kernels, reduce(): pl.pallas_call(functools.partial(reduce_kernel, with_values), out_shape=o...  193 us
    pallas_call x3, Pallas kernels, gather(): pl.pallas_call(functools.partial(gather_kernel, with_values), out_shape=o...  176 us
    dot_general x32, matrix products, dot(): return jnp.einsum(spec, left, right, preferred_element_type=f32)  63.2 us
    pallas_call x4, Pallas kernels, trade(): pl.pallas_call(functools.partial(trade_kernel, to_rows), out_shape=jax.Sh...  48.1 us
    unnamed x189, local copies, waits for them, and re-layouts  24.1 us
    slice x5, local copies, waits for them, and re-layouts, from_slices(): return packed[:, low:low + rows].reshape(-1, width)  21.8 us
  transfers between devices with their start and end apart: 3, of which 0 were waited for; matrix products, arithmetic and copies ran while one was open for 7% of the time, Pallas kernels for 18%

profile of v2, /device:TPU:0, one launch (start us, length us, event | category | flops | bytes accessed | tf_op | source)
XLA Modules:
  0.0 590.8 jit_solution(14944194032662448868)
XLA Ops:
  6.5 33.8 %shard_map.169 = bf16[32,32,768]{2,1,0:T(8,128)(2,1)} custom-call(bf16[32,768]{1,0:T(8,128)(2,1)} %fusion.75.own), custom_call_target="tpu_custom_call" | custom-call | tf_op jit(solution)/shard_map/pallas_call | solution.py:322
  50.4 71.1 %shard_map.170 = (bf16[32,240,768]{2,1,0:T(8,128)(2,1)}, bf16[3,512,1024]{2,1,0:T(8,128)(2,1)}) custom-call(bf16[240,768]{1,0:T(8,128)(2,1)} %constant_dynamic-update-slice_fusion.own, bf16[4,3,64,256]{3,2,1,0:T(8,128)(2,1)} %bitcast.269), custom_call_target="tpu_custom_call" | custom-call | tf_op jit(solution)/shard_map/pallas_call | solution.py:322
  121.6 4.8 slice.234
  127.4 5.8 fusion.99
  136.3 10.2 %shard_map.171 = bf16[4,3,64,256]{3,2,1,0:T(8,128)(2,1)} custom-call(bf16[3,8,64,128]{3,2,1,0:T(8,128)(2,1)} %multiply_convert_fusion.12.source), custom_call_target="tpu_custom_call" | custom-call | tf_op jit(solution)/shard_map/pallas_call | solution.py:727
  149.8 3.0 fusion.23
  156.3 71.5 %shard_map.172 = (bf16[32,216,768]{2,1,0:T(8,128)(2,1)}, bf16[3,512,1024]{2,1,0:T(8,128)(2,1)}) custom-call(bf16[216,768]{1,0:T(8,128)(2,1)} %get-tuple-element.73.own, bf16[4,3,64,256]{3,2,1,0:T(8,128)(2,1)} %bitcast.249), custom_call_target="tpu_custom_call" | custom-call | tf_op jit(solution)/shard_map/pallas_call | solution.py:322
  227.8 5.0 fusion.100
  232.8 4.9 slice.251
  240.8 10.9 %shard_map.173 = bf16[4,3,64,256]{3,2,1,0:T(8,128)(2,1)} custom-call(bf16[3,8,64,128]{3,2,1,0:T(8,128)(2,1)} %multiply_convert_fusion.8.source), custom_call_target="tpu_custom_call" | custom-call | tf_op jit(solution)/shard_map/pallas_call | solution.py:727
  257.7 3.6 fusion
  278.1 10.4 %shard_map.174 = bf16[3,8,64,128]{3,2,1,0:T(8,128)(2,1)} custom-call(bf16[4,3,64,256]{3,2,1,0:T(8,128)(2,1)} %bitcast.244), custom_call_target="tpu_custom_call" | custom-call | tf_op jit(solution)/shard_map/pallas_call | solution.py:727
  290.6 3.8 multiply_convert_fusion.1.refs_0_
  294.4 90.0 %shard_map.175 = (f32[224,768]{1,0:T(8,128)}, bf16[4,3,64,256]{3,2,1,0:T(8,128)(2,1)}) custom-call(bf16[32,224,768]{2,1,0:T(8,128)(2,1)} %broadcast_dynamic-update-slice_fusion.packed, bf16[3,512,1024]{2,1,0:T(8,128)(2,1)} %multiply_convert_fusion.1.refs_0_), custom_call_target="tpu_custom_call" | custom-call | tf_op jit(solution)/shard_map/pallas_call | solution.py:631
  386.7 5.0 fusion.1
  394.8 4.4 convolution_convert_fusion
  406.2 16.7 %shard_map.176 = bf16[3,8,64,128]{3,2,1,0:T(8,128)(2,1)} custom-call(bf16[4,3,64,256]{3,2,1,0:T(8,128)(2,1)} %bitcast.245), custom_call_target="tpu_custom_call" | custom-call | tf_op jit(solution)/shard_map/pallas_call | solution.py:727
  431.1 5.0 constant_dynamic-update-slice_fusion.18
  439.9 81.8 %shard_map.177 = (f32[240,768]{1,0:T(8,128)}, bf16[4,3,64,256]{3,2,1,0:T(8,128)(2,1)}) custom-call(bf16[32,240,768]{2,1,0:T(8,128)(2,1)} %constant_dynamic-update-slice_fusion.17.packed, bf16[3,512,1024]{2,1,0:T(8,128)(2,1)} %multiply_convert_fusion.refs_0_), custom_call_target="tpu_custom_call" | custom-call | tf_op jit(solution)/shard_map/pallas_call | solution.py:631
  526.9 21.5 %shard_map.178 = f32[32,768]{1,0:T(8,128)} custom-call(bf16[32,32,768]{2,1,0:T(8,128)(2,1)} %fusion.15.packed), custom_call_target="tpu_custom_call" | custom-call | tf_op jit(solution)/shard_map/pallas_call | solution.py:631
  559.3 3.9 multiply_convert_fusion.4
  563.1 7.4 %collective-permute-start.2 = (bf16[3,128,1024]{2,1,0:T(8,128)(2,1)}, bf16[3,128,1024]{2,1,0:T(8,128)(2,1)}, u32[]{:S(2)}, u32[]{:S(2)}) collective-permute-start(bf16[3,128,1024]{2,1,0:T(8,128)(2,1)} %multiply_convert_fusion.4), channel_id=1, source_target_pairs={{0,0},{1,4},{2,2},{3,6},{4,1},{5,5},{6,3},{7,7},{8,8},{9,12},{10,1... | collective-permute-start | bytes 2359304 | tf_op jit(solution)/shard_map/ppermute | solution.py:1046
  582.5 5.1 fusion.17
  587.5 3.0 maximum_convert_fusion
  (291 shorter events, 105.6 us)
Async XLA Ops:
  0.6 42.4 %copy-start.60 = (bf16[2,24,768]{2,1,0:T(8,128)(2,1)S(1)}, bf16[2,24,768]{2,1,0:T(8,128)(2,1)}, u32[]{:S(2)}) copy-start(bf16[2,24,768]{2,1,0:T(8,128)(2,1)} %param.15) | copy-start | bytes 221188
  0.7 44.8 %copy-start.21 = (bf16[1,256,768]{2,1,0:T(8,128)(2,1)S(1)}, bf16[1,256,768]{2,1,0:T(8,128)(2,1)}, u32[]{:S(2)}) copy-start(bf16[1,256,768]{2,1,0:T(8,128)(2,1)} %param.10) | copy-start | bytes 1179652
  0.7 132.5 %collective-permute-start = (bf16[2,3,128,1024]{3,2,1,0:T(8,128)(2,1)}, bf16[2,3,128,1024]{3,2,1,0:T(8,128)(2,1)S(1)}, u32[]{:S(2)}, u32[]{:S(2)}) collective-permute-start(bf16[2,3,128,1024]{3,2,1,0:T(8,128)(2,1)} %param.14), channel_id=1, source_target_pairs={{0,0},{1,4},{2,2},{3,6},{4,1},{5,5},{6,3},{7,7},{8,8},{9,12},{10,1... | collective-permute-start | bytes 4718600 | tf_op jit(solution)/shard_map/ppermute | solution.py:957
  41.7 79.9 %copy-start.40 = (bf16[32,24,768]{2,1,0:T(8,128)(2,1)}, bf16[32,24,768]{2,1,0:T(8,128)(2,1)S(1)}, u32[]{:S(2)}) copy-start(bf16[32,24,768]{2,1,0:T(8,128)(2,1)S(1)} %slice.220) | copy-start | bytes 3538948
  45.4 81.0 %copy-start.63 = (f32[768]{0:T(1024)}, f32[768]{0:T(1024)S(1)}, u32[]{:S(2)}) copy-start(f32[768]{0:T(1024)S(1)} %mul.454) | copy-start | bytes 9220
  45.7 80.7 %copy-start.70 = (f32[256]{0:T(256)}, f32[256]{0:T(256)S(1)}, u32[]{:S(2)}) copy-start(f32[256]{0:T(256)S(1)} %add_rsqrt_fusion.3) | copy-start | bytes 3076
  133.2 21.8 %copy-start.2 = (bf16[32,24,768]{2,1,0:T(8,128)(2,1)}, bf16[32,24,768]{2,1,0:T(8,128)(2,1)S(1)}, u32[]{:S(2)}) copy-start(bf16[32,24,768]{2,1,0:T(8,128)(2,1)S(1)} %get-tuple-element.39) | copy-start | bytes 3538948
  133.2 104.8 %copy-start.6 = (bf16[2,3,128,1024]{3,2,1,0:T(8,128)(2,1)}, bf16[2,3,128,1024]{3,2,1,0:T(8,128)(2,1)S(1)}, u32[]{:S(2)}) copy-start(bf16[2,3,128,1024]{3,2,1,0:T(8,128)(2,1)S(1)} %collective-permute-done) | copy-start | bytes 4718596
  240.8 14.8 %copy-start.36 = (bf16[32,24,768]{2,1,0:T(8,128)(2,1)S(1)}, bf16[32,24,768]{2,1,0:T(8,128)(2,1)}, u32[]{:S(2)}) copy-start(bf16[32,24,768]{2,1,0:T(8,128)(2,1)} %get-tuple-element.45) | copy-start | bytes 3538948
  274.8 13.8 %copy-start.26 = (f32[3,512,128]{2,1,0:T(8,128)S(1)}, f32[3,512,128]{2,1,0:T(8,128)}, u32[]{:S(2)}) copy-start(f32[3,512,128]{2,1,0:T(8,128)} %copy-done.25) | copy-start | bytes 2359300
  274.8 13.8 %copy-start.59 = (f32[3,8,128]{2,1,0:T(8,128)S(1)}, f32[3,8,128]{2,1,0:T(8,128)}, u32[]{:S(2)}) copy-start(f32[3,8,128]{2,1,0:T(8,128)} %copy-done.58) | copy-start | bytes 36868
  274.8 15.6 %copy-start.55 = (f32[8,1024]{1,0:T(8,128)S(1)}, f32[8,1024]{1,0:T(8,128)}, u32[]{:S(2)}) copy-start(f32[8,1024]{1,0:T(8,128)} %fusion.77) | copy-start | bytes 98308
  294.4 90.0 %copy-start.3 = (bf16[32,24,768]{2,1,0:T(8,128)(2,1)S(1)}, bf16[32,24,768]{2,1,0:T(8,128)(2,1)}, u32[]{:S(2)}) copy-start(bf16[32,24,768]{2,1,0:T(8,128)(2,1)} %copy-done.2) | copy-start | bytes 3538948
  294.4 90.0 %copy-start.67 = (f32[256]{0:T(256)S(1)}, f32[256]{0:T(256)}, u32[]{:S(2)}) copy-start(f32[256]{0:T(256)} %copy-done.66) | copy-start | bytes 3076
  404.0 18.9 %copy-start.57 = (f32[3,8,128]{2,1,0:T(8,128)S(1)}, f32[3,8,128]{2,1,0:T(8,128)}, u32[]{:S(2)}) copy-start(f32[3,8,128]{2,1,0:T(8,128)} %copy-done.56) | copy-start | bytes 36868
  439.9 81.9 %copy-start.22 = (bf16[1,256,768]{2,1,0:T(8,128)(2,1)S(1)}, bf16[1,256,768]{2,1,0:T(8,128)(2,1)}, u32[]{:S(2)}) copy-start(bf16[1,256,768]{2,1,0:T(8,128)(2,1)} %param.10) | copy-start | bytes 1179652
  439.9 81.9 %copy-start.41 = (bf16[32,24,768]{2,1,0:T(8,128)(2,1)S(1)}, bf16[32,24,768]{2,1,0:T(8,128)(2,1)}, u32[]{:S(2)}) copy-start(bf16[32,24,768]{2,1,0:T(8,128)(2,1)} %copy-done.40) | copy-start | bytes 3538948
  439.9 81.9 %copy-start.64 = (f32[768]{0:T(1024)S(1)}, f32[768]{0:T(1024)}, u32[]{:S(2)}) copy-start(f32[768]{0:T(1024)} %copy-done.63) | copy-start | bytes 9220
  439.9 81.9 %copy-start.71 = (f32[256]{0:T(256)S(1)}, f32[256]{0:T(256)}, u32[]{:S(2)}) copy-start(f32[256]{0:T(256)} %copy-done.70) | copy-start | bytes 3076
  525.5 32.8 %copy-start.61 = (f32[3,8,128]{2,1,0:T(8,128)S(1)}, f32[3,8,128]{2,1,0:T(8,128)}, u32[]{:S(2)}) copy-start(f32[3,8,128]{2,1,0:T(8,128)} %get-tuple-element.71) | copy-start | bytes 36868
  525.5 32.8 %copy-start.75 = (s32[8]{0:T(128)S(1)}, s32[8]{0:T(128)}, u32[]{:S(2)}) copy-start(s32[8]{0:T(128)} %copy-done.73) | copy-start | bytes 100
  526.9 32.3 %copy-start.8 = (bf16[2,3,128,1024]{3,2,1,0:T(8,128)(2,1)S(1)}, bf16[2,3,128,1024]{3,2,1,0:T(8,128)(2,1)}, u32[]{:S(2)}) copy-start(bf16[2,3,128,1024]{3,2,1,0:T(8,128)(2,1)} %copy-done.6) | copy-start | bytes 4718596
  563.1 24.4 %collective-permute-start.2 = (bf16[3,128,1024]{2,1,0:T(8,128)(2,1)}, bf16[3,128,1024]{2,1,0:T(8,128)(2,1)}, u32[]{:S(2)}, u32[]{:S(2)}) collective-permute-start(bf16[3,128,1024]{2,1,0:T(8,128)(2,1)} %multiply_convert_fusion.4), channel_id=1, source_target_pairs={{0,0},{1,4},{2,2},{3,6},{4,1},{5,5},{6,3},{7,7},{8,8},{9,12},{10,1... | collective-permute-start | bytes 2359304 | tf_op jit(solution)/shard_map/ppermute | solution.py:1046
  573.5 14.1 %collective-permute-start.1 = (bf16[3,128,1024]{2,1,0:T(8,128)(2,1)}, bf16[3,128,1024]{2,1,0:T(8,128)(2,1)S(1)}, u32[]{:S(2)}, u32[]{:S(2)}) collective-permute-start(bf16[3,128,1024]{2,1,0:T(8,128)(2,1)} %multiply_convert_fusion.5), channel_id=1, source_target_pairs={{0,0},{1,4},{2,2},{3,6},{4,1},{5,5},{6,3},{7,7},{8,8},{9,12},{10,1... | collective-permute-start | bytes 2359304 | tf_op jit(solution)/shard_map/ppermute | solution.py:1046
  (63 other events, 308.3 us)
